TPU v7x, 256 devices: a whole 4x4x8 slice. The times are simulated.
256 devices in a mesh: layer: 128 (over z, y, x), batch: 2 (over core).
Axes of the slice: x: 4, y: 4, z: 8, core: 2. Of those that a mesh axis runs over, the one named last changes fastest.
Arguments:
- kernels: bfloat16 [512, 9, 128, 128], P('layer'), may hold values from -0.1875 to 0.1875
- biases: float32 [512, 128], P('layer'), may hold values from -3 to 3
- states: float32 [128, 2, 16, 16, 128], P('layer', 'batch'), may hold values from -6 to 6
- adjoint_guess: float32 [128, 2, 16, 16, 128], P('layer', 'batch'), may hold values from -6 to 6
Outputs:
- new_states: float32 [128, 2, 16, 16, 128], P('layer', 'batch')
- new_ends: float32 [128, 2, 16, 16, 128], P('layer', 'batch')
- new_adjoint: float32 [128, 2, 16, 16, 128], P('layer', 'batch')
- new_back_starts: float32 [128, 2, 16, 16, 128], P('layer', 'batch')
- grad_kernel: float32 [512, 9, 128, 128], P('layer')
- grad_bias: float32 [512, 128], P('layer')
All inputs are finite; a program needn't handle non-finite values.
Results may differ from a plain program's by a relative error of at most 0.0094.
Values sent between devices are 32-bit elements; how exact they have to be, the bound alone decides.
A program may use at most 128 MiB of HBM per device.

v0:
```python
import jax
import jax.numpy as jnp
from jax import lax
from jax.sharding import Mesh
from jax.sharding import PartitionSpec as P

LAYER = ("layer_0", "layer_1", "layer_2")


STEP_SIZE = 0.1


def from_behind(value, axis, steps):
    count = lax.axis_size(axis)
    leading, last = (max(0, -steps), min(count, count - steps))
    return lax.ppermute(value, axis, [(source, source + steps) for source in range(leading, last)])


def nothing_yet(shard, identity):
    return jax.tree.map(
        lambda part, zero: jnp.zeros_like(part) + jnp.asarray(zero, part.dtype), shard, identity
    )


def prefix_by_axis(shard, axes, combine, identity, reverse):
    before = start = nothing_yet(shard, identity)
    subtotal = shard
    for axis in reversed(axes):
        peers, mine = (lax.axis_size(axis), lax.axis_index(axis))
        pieces = jax.tree.map(lambda part: lax.all_gather(part, axis), subtotal)
        inside, subtotal = (start, start)
        for k in reversed(range(peers)) if reverse else range(peers):
            passed = k > mine if reverse else k < mine
            subtotal = combine(subtotal, jax.tree.map(lambda part: part[k], pieces))
            inside = jax.tree.map(lambda new, old: jnp.where(passed, new, old), subtotal, inside)
        before = combine(inside, before)
    return before


def copy_for_each(shard, axis):
    peers = lax.axis_size(axis)
    return lax.all_to_all(
        jnp.broadcast_to(shard[None], (peers, *shard.shape)), axis, 0, 0, tiled=True
    )


def taken_together(shard, axis):
    return copy_for_each(shard, axis).sum(axis=0)


def together(arrays, axis):
    vector, at, outs = (jnp.concatenate([a.reshape(-1) for a in arrays]), 0, [])
    subtotal = taken_together(vector, axis)
    for a in arrays:
        outs.append(subtotal[at : at + a.size].reshape(a.shape))
        at += a.size
    return tuple(outs)


def patches(image):
    extent = image.shape[1]
    padded = jnp.pad(image, ((0, 0), (1, 1), (1, 1), (0, 0)))
    shifted = [
        padded[:, row_shift : row_shift + extent, col_shift : col_shift + extent, :]
        for row_shift in range(3)
        for col_shift in range(3)
    ]
    return jnp.concatenate(shifted, axis=-1)


def convolve(image, weights_flat):
    return jnp.dot(patches(image), weights_flat, preferred_element_type=jnp.float32)


def forward_step(state, weights_flat, bias_row):
    pre_act = convolve(state.astype(jnp.bfloat16), weights_flat) + bias_row
    return state + STEP_SIZE * jnp.tanh(pre_act)


def adjoint_step(adjoint, slope, flipped):
    sens = (slope * adjoint).astype(jnp.bfloat16)
    return adjoint + STEP_SIZE * convolve(sens, flipped)


def full_dot(left, right):
    return jnp.dot(left, right, precision=lax.Precision.HIGHEST, preferred_element_type=jnp.float32)


def compose(earlier, later):
    first_map, first_field = earlier
    second_map, second_field = later
    return (full_dot(first_map, second_map), full_dot(first_field, second_map) + second_field)


def body(kernels, biases, states, adjoint_guess):
    count = kernels.shape[0]
    channels = kernels.shape[2]
    position = lax.axis_index(LAYER)
    intervals = lax.axis_size(LAYER)
    weights_all = kernels.reshape(count, 9 * channels, channels)
    flipped_all = jnp.transpose(kernels[:, ::-1], (0, 1, 3, 2)).reshape(
        count, 9 * channels, channels
    )
    unit = jnp.eye(channels, dtype=jnp.float32)
    centre = kernels[0, 4].astype(jnp.float32)
    guess = states[0]
    zero_field = jnp.zeros(guess.shape, jnp.float32)
    zero_map = jnp.zeros((channels, channels), jnp.float32)

    def relax_once(state):
        for offset in range(count - 1):
            state = forward_step(state, weights_all[offset], biases[offset])
        return forward_step(state, weights_all[count - 1], biases[count - 1])

    relaxed = relax_once(guess)
    received = from_behind(relaxed, LAYER, 1)
    start = jnp.where(position == 0, guess, received)
    coarse = jnp.where(position == 0, zero_map, unit + count * STEP_SIZE * centre)
    carry_term = relax_once(start) - full_dot(start, coarse)
    combined = prefix_by_axis((coarse, carry_term), LAYER, compose, (unit, zero_field), False)[1]
    new_states = jnp.where(position == 0, guess, combined)
    new_ends = full_dot(new_states, coarse) + carry_term
    state = new_states
    block_inputs = []
    slopes = []
    for offset in range(count):
        rounded = state.astype(jnp.bfloat16)
        activ = jnp.tanh(convolve(rounded, weights_all[offset]) + biases[offset])
        block_inputs.append(rounded)
        slopes.append(1.0 - activ * activ)
        state = state + STEP_SIZE * activ
    lam_guess = adjoint_guess[0]

    def back_relax(adjoint):
        for offset in range(count - 1, 0, -1):
            adjoint = adjoint_step(adjoint, slopes[offset], flipped_all[offset])
        return adjoint_step(adjoint, slopes[0], flipped_all[0])

    back_relaxed = back_relax(lam_guess)
    back_received = from_behind(back_relaxed, LAYER, -1)
    back_start = jnp.where(position == intervals - 1, lam_guess, back_received)
    back_coarse = jnp.where(
        position == intervals - 1, zero_map, unit + count * STEP_SIZE * jnp.transpose(centre)
    )
    back_carry_term = back_relax(back_start) - full_dot(back_start, back_coarse)
    back_combined = prefix_by_axis(
        (back_coarse, back_carry_term), LAYER, compose, (unit, zero_field), True
    )[1]
    new_adjoint = jnp.where(position == intervals - 1, lam_guess, back_combined)
    new_back_starts = full_dot(new_adjoint, back_coarse) + back_carry_term
    factor = STEP_SIZE / (guess.shape[0] * lax.axis_size("batch") * guess.shape[1] * guess.shape[2])
    adjoint = new_adjoint
    kernel_terms = [None] * count
    bias_terms = [None] * count
    for offset in range(count - 1, -1, -1):
        sens = (slopes[offset] * adjoint).astype(jnp.bfloat16)
        kernel_part = jnp.einsum(
            "bhwk,bhwc->kc", patches(block_inputs[offset]), sens, preferred_element_type=jnp.float32
        )
        bias_part = jnp.sum(sens.astype(jnp.float32), axis=(0, 1, 2))
        kernel_terms[offset] = kernel_part
        bias_terms[offset] = bias_part
        if offset > 0:
            adjoint = adjoint + STEP_SIZE * convolve(sens, flipped_all[offset])
    kernel_stack = jnp.stack(kernel_terms)
    bias_stack = jnp.stack(bias_terms)
    kernel_stack, bias_stack = together((kernel_stack, bias_stack), "batch")
    grad_kernel = (factor * kernel_stack).reshape(count, 9, channels, channels)
    grad_bias = factor * bias_stack
    return (
        new_states[None],
        new_ends[None],
        new_adjoint[None],
        new_back_starts[None],
        grad_kernel,
        grad_bias,
    )


def solution(mesh):
    torus = Mesh(
        mesh.devices.reshape(8, 4, 4, mesh.shape["batch"]),
        ("layer_0", "layer_1", "layer_2", "batch"),
    )
    placed = (
        P(LAYER, None, None, None),
        P(LAYER, None),
        P(LAYER, "batch", None, None, None),
        P(LAYER, "batch", None, None, None),
    )
    return jax.shard_map(
        body,
        mesh=torus,
        in_specs=placed,
        out_specs=(
            P(LAYER, "batch", None, None, None),
            P(LAYER, "batch", None, None, None),
            P(LAYER, "batch", None, None, None),
            P(LAYER, "batch", None, None, None),
            P(LAYER, None, None, None),
            P(LAYER, None),
        ),
        check_vma=False,
    )
```

profile of v0, /device:TPU:1, one launch (start us, length us, event | category | flops | bytes accessed | tf_op | source)
XLA Modules:
  0.0 311.9 jit_solution(17752702603916360218)
XLA Ops:
  7.2 0.8 slice_bitcast_fusion.40
  8.1 0.9 bitcast_convert_fusion
  9.1 0.9 constant_dynamic-update-slice_fusion.4
  10.2 1.3 fusion.292
  13.4 1.0 fusion.42
  14.4 4.6 %collective-permute-start = (f32[1,16,16,128]{3,2,1,0:T(8,128)}, f32[1,16,16,128]{3,2,1,0:T(8,128)}, u32[]{:S(2)}, u32[]{:S(2)}) collective-permute-start(f32[1,16,16,128]{3,2,1,0:T(8,128)} %fusion.42), channel_id=1, source_target_pairs={{0,2},{2,4},{4,6},{6,8},{8,10},{10,12},{12,14},{14,16},{16,18},{18... | collective-permute-start | bytes 393224 | tf_op jit(solution)/shard_map/ppermute | solution.py:16
  19.0 0.6 slice.887
  19.8 0.9 copy.51
  20.8 9.9 %all_gather.70 = f32[4,128,128]{2,1,0:T(8,128)S(1)} all-gather(f32[1,128,128]{2,1,0:T(8,128)S(1)} %copy.38), channel_id=1, replica_groups=mesh['layer_0'=8,'layer_1'=4,'layer_2'=4,'batch'=2] {'layer_2'}, dimensions={0}, use_global_device_ids=true | all-gather | bytes 327680 | tf_op jit(solution)/shard_map/all_gather | solution.py:30
  30.9 0.6 copy-done.41
  32.2 10.4 %all-gather = f32[512,128]{1,0:T(8,128)} all-gather(f32[128,128]{1,0:T(8,128)S(1)} %fusion.165), channel_id=2, replica_groups=mesh['layer_0'=8,'layer_1'=4,'layer_2'=4,'batch'=2] {'layer_1'}, dimensions={0}, use_global_device_ids=true | all-gather | bytes 327680 | tf_op jit(solution)/shard_map/all_gather | solution.py:30
  42.5 9.4 %all-gather.5 = f32[512,128]{1,0:T(8,128)S(1)} all-gather(f32[128,128]{1,0:T(8,128)S(1)} %fusion.133), channel_id=7, replica_groups=mesh['layer_0'=8,'layer_1'=4,'layer_2'=4,'batch'=2] {'layer_2'}, dimensions={0}, use_global_device_ids=true | all-gather | bytes 327680 | tf_op jit(solution)/shard_map/all_gather | solution.py:30
  52.9 0.6 copy-done.34
  53.5 0.8 fusion.217
  54.4 0.8 fusion.291
  55.9 1.2 copy.41
  57.1 0.8 fusion.177
  60.7 10.0 %all-gather.2 = f32[4,16,16,128]{3,2,1,0:T(8,128)S(1)} all-gather(f32[1,16,16,128]{3,2,1,0:T(8,128)S(1)} %fusion.98), channel_id=4, replica_groups=mesh['layer_0'=8,'layer_1'=4,'layer_2'=4,'batch'=2] {'layer_2'}, dimensions={0}, use_global_device_ids=true | all-gather | bytes 655360 | tf_op jit(solution)/shard_map/all_gather | solution.py:30
  71.0 0.6 copy-done.14
  72.5 11.9 %all-gather.3 = f32[64,16,128]{2,1,0:T(8,128)S(1)} all-gather(f32[16,16,128]{2,1,0:T(8,128)S(1)} %convolution_add_fusion.42), channel_id=5, replica_groups=mesh['layer_0'=8,'layer_1'=4,'layer_2'=4,'batch'=2] {'layer_1'}, dimensions={0}, use_global_device_ids=true | all-gather | bytes 655360 | tf_op jit(solution)/shard_map/all_gather | solution.py:30
  84.7 0.6 copy-done.17
  85.9 0.9 convolution_add_fusion.39
  86.9 10.1 %all-gather.6 = f32[512,128]{1,0:T(8,128)S(1)} all-gather(f32[128,128]{1,0:T(8,128)S(1)} %copy-done.36), channel_id=8, replica_groups=mesh['layer_0'=8,'layer_1'=4,'layer_2'=4,'batch'=2] {'layer_1'}, dimensions={0}, use_global_device_ids=true | all-gather | bytes 327680 | tf_op jit(solution)/shard_map/all_gather | solution.py:30
  97.0 1.0 fusion.234
  99.0 25.8 %all-gather.1 = f32[1024,128]{1,0:T(8,128)} all-gather(f32[128,128]{1,0:T(8,128)S(1)} %fusion.228), channel_id=3, replica_groups=mesh['layer_0'=8,'layer_1'=4,'layer_2'=4,'batch'=2] {'layer_0'}, dimensions={0}, use_global_device_ids=true | all-gather | bytes 589824 | tf_op jit(solution)/shard_map/all_gather | solution.py:30
  125.3 10.8 %all-gather.14.cloned.1.call-done = f32[128,16,128]{2,1,0:T(8,128)} async-done(((f32[16,16,128]{2,1,0:T(8,128)}), f32[128,16,128]{2,1,0:T(8,128)}) %all-gather.14.cloned.1.call-update) | async-done | bytes 1048592 | tf_op jit(solution)/shard_map/all_gather | solution.py:30
  136.0 1.2 convolution_add_fusion.47
  137.2 1.2 convolution_add_fusion.38
  138.5 1.2 convolution_add_fusion.37
  139.7 1.2 convolution_add_fusion.36
  140.9 1.2 convolution_add_fusion.35
  142.1 1.2 convolution_add_fusion.34
  143.3 1.2 convolution_add_fusion.33
  144.5 1.2 fusion.44
  151.3 1.3 collective-permute-start.1
  152.6 0.8 fusion.174
  153.4 3.8 %collective-permute-done.1 = f32[1,16,16,128]{3,2,1,0:T(8,128)S(1)} collective-permute-done((f32[1,16,16,128]{3,2,1,0:T(8,128)S(1)}, f32[1,16,16,128]{3,2,1,0:T(8,128)S(1)}, u32[]{:S(2)}, u32[]{:S(2)}) %collective-permute-start.1) | collective-permute-done | bytes 131104 | tf_op jit(solution)/shard_map/ppermute | solution.py:16
  160.0 10.6 %all-gather.8 = f32[4,16,16,128]{3,2,1,0:T(8,128)S(1)} all-gather(f32[1,16,16,128]{3,2,1,0:T(8,128)S(1)} %fusion.89), channel_id=10, replica_groups=mesh['layer_0'=8,'layer_1'=4,'layer_2'=4,'batch'=2] {'layer_2'}, dimensions={0}, use_global_device_ids=true | all-gather | bytes 655360 | tf_op jit(solution)/shard_map/all_gather | solution.py:30
  171.7 12.0 %all-gather.9 = f32[64,16,128]{2,1,0:T(8,128)S(1)} all-gather(f32[16,16,128]{2,1,0:T(8,128)S(1)} %convolution_add_fusion.24), channel_id=11, replica_groups=mesh['layer_0'=8,'layer_1'=4,'layer_2'=4,'batch'=2] {'layer_1'}, dimensions={0}, use_global_device_ids=true | all-gather | bytes 655360 | tf_op jit(solution)/shard_map/all_gather | solution.py:30
  184.1 0.6 copy-done.18
  185.2 0.9 convolution_add_fusion.21
  186.2 1.1 fusion.212
  187.7 1.0 fusion.141
  188.8 1.1 convolution_bitcast_fusion.8
  189.9 20.4 %all-gather.7 = f32[1024,128]{1,0:T(8,128)S(1)} all-gather(f32[128,128]{1,0:T(8,128)S(1)} %fusion.206), channel_id=9, replica_groups=mesh['layer_0'=8,'layer_1'=4,'layer_2'=4,'batch'=2] {'layer_0'}, dimensions={0}, use_global_device_ids=true | all-gather | bytes 589824 | tf_op jit(solution)/shard_map/all_gather | solution.py:30
  210.3 1.8 fusion.49
  212.4 0.9 convolution_add_fusion.12
  213.3 27.0 %all-gather.16.cloned.1.call-done = f32[128,16,128]{2,1,0:T(8,128)} async-done(((f32[16,16,128]{2,1,0:T(8,128)}), f32[128,16,128]{2,1,0:T(8,128)}) %all-gather.16.cloned.1.call-update) | async-done | bytes 1048592 | tf_op jit(solution)/shard_map/all_gather | solution.py:30
  240.2 1.2 convolution_add_fusion.29
  241.4 1.2 convolution_add_fusion.20
  242.6 1.2 convolution_add_fusion.19
  243.9 1.2 convolution_add_fusion.18
  245.0 1.2 convolution_add_fusion.17
  246.2 1.2 convolution_add_fusion.16
  247.4 1.2 convolution_add_fusion.15
  248.6 1.2 fusion.46
  250.1 0.9 fusion.51
  252.1 0.4 convolution_bitcast_fusion.1
  254.2 0.4 convolution_bitcast_fusion.3
  254.9 11.2 %broadcast_in_dim.36 = f32[2,1,590336]{2,1,0:T(1,128)S(1)} broadcast(f32[590336]{0:T(1024)S(1)} %pad_maximum_fusion), dimensions={2} | broadcast | bytes 7084032 | tf_op jit(solution)/shard_map/broadcast_in_dim | solution.py:43
  266.1 13.7 %all_to_all.6 = f32[2,1,590336]{2,1,0:T(1,128)} all-to-all(f32[2,1,590336]{2,1,0:T(1,128)S(1)} %broadcast_in_dim.36), channel_id=1, replica_groups=mesh['layer_0'=8,'layer_1'=4,'layer_2'=4,'batch'=2] {'batch'}, dimensions={0} | all-to-all | bytes 9445376 | tf_op jit(solution)/shard_map/all_to_all | solution.py:42
  279.7 23.1 %reduce_sum.49 = f32[590336]{0:T(1024)S(1)} reduce(f32[2,1,590336]{2,1,0:T(1,128)} %all_to_all.6, f32[]{:T(128)} %constant.13.clone.1), dimensions={0,1}, to_apply=%region_4.5 | reduce | flops 590336 | bytes 7084036 | tf_op jit(solution)/shard_map/reduce_sum | solution.py:48
  302.9 0.6 fusion.269
  303.5 1.6 slice_multiply_fusion
  (373 shorter events, 24.1 us)
Async XLA Ops:
  7.2 4.3 %copy-start.2 = (f32[1,1,16,16,128]{4,3,2,1,0:T(8,128)S(1)}, f32[1,1,16,16,128]{4,3,2,1,0:T(8,128)}, u32[]{:S(2)}) copy-start(f32[1,1,16,16,128]{4,3,2,1,0:T(8,128)} %param.6) | copy-start | bytes 393220
  7.2 128.9 %all-gather.14.cloned.1.call-start = ((), (), s32[]{:S(2)}) async-start(), calls=%async_computation.1 | async-start | bytes 1179648 | tf_op jit(solution)/shard_map/all_gather | solution.py:30
  12.6 6.4 %copy-start.1 = (bf16[4,9,128,128]{3,2,1,0:T(8,128)(2,1)S(1)}, bf16[4,9,128,128]{3,2,1,0:T(8,128)(2,1)}, u32[]{:S(2)}) copy-start(bf16[4,9,128,128]{3,2,1,0:T(8,128)(2,1)} %param.4) | copy-start | bytes 3538948
  14.4 43.4 %collective-permute-start = (f32[1,16,16,128]{3,2,1,0:T(8,128)}, f32[1,16,16,128]{3,2,1,0:T(8,128)}, u32[]{:S(2)}, u32[]{:S(2)}) collective-permute-start(f32[1,16,16,128]{3,2,1,0:T(8,128)} %fusion.42), channel_id=1, source_target_pairs={{0,2},{2,4},{4,6},{6,8},{8,10},{10,12},{12,14},{14,16},{16,18},{18... | collective-permute-start | bytes 393224 | tf_op jit(solution)/shard_map/ppermute | solution.py:16
  20.6 139.1 %copy-start.10 = (bf16[1,1,128,128]{2,3,1,0:T(8,128)(2,1)}, bf16[1,1,128,128]{2,3,1,0:T(8,128)(2,1)S(1)}, u32[]{:S(2)}) copy-start(bf16[1,1,128,128]{2,3,1,0:T(8,128)(2,1)S(1)} %copy.51) | copy-start | bytes 98308
  30.7 1.5 copy-start.7
  30.9 0.6 copy-start.41
  31.7 20.2 %copy-start.37 = (f32[128,128]{1,0:T(8,128)}, f32[128,128]{1,0:T(8,128)S(1)}, u32[]{:S(2)}) copy-start(f32[128,128]{1,0:T(8,128)S(1)} %fusion.169) | copy-start | bytes 196612
  31.9 20.2 %copy-start.38 = (f32[128,128]{1,0:T(8,128)}, f32[128,128]{1,0:T(8,128)S(1)}, u32[]{:S(2)}) copy-start(f32[128,128]{1,0:T(8,128)S(1)} %fusion.167) | copy-start | bytes 196612
  32.1 20.4 %copy-start.39 = (f32[128,128]{1,0:T(8,128)}, f32[128,128]{1,0:T(8,128)S(1)}, u32[]{:S(2)}) copy-start(f32[128,128]{1,0:T(8,128)S(1)} %fusion.165) | copy-start | bytes 196612
  51.9 0.7 copy-start.4
  52.1 0.6 copy-start.40
  52.3 0.6 copy-start.32
  52.9 0.6 copy-start.34
  54.4 3.5 %copy-start.3 = (f32[1,1,16,16,128]{4,3,2,1,0:T(8,128)S(1)}, f32[1,1,16,16,128]{4,3,2,1,0:T(8,128)}, u32[]{:S(2)}) copy-start(f32[1,1,16,16,128]{4,3,2,1,0:T(8,128)} %param.6) | copy-start | bytes 393220
  55.2 1.9 copy-start.6
  59.4 11.4 %copy-start.8 = (f32[4,128,128]{2,1,0:T(8,128)S(1)}, f32[4,128,128]{2,1,0:T(8,128)}, u32[]{:S(2)}) copy-start(f32[4,128,128]{2,1,0:T(8,128)} %copy-done.7) | copy-start | bytes 786436
  60.7 10.1 %copy-start.20 = (f32[1,16,16,128]{3,2,1,0:T(8,128)}, f32[1,16,16,128]{3,2,1,0:T(8,128)S(1)}, u32[]{:S(2)}) copy-start(f32[1,16,16,128]{3,2,1,0:T(8,128)S(1)} %fusion.98) | copy-start | bytes 393220
  60.7 26.2 %copy-start.36 = (f32[128,128]{1,0:T(8,128)S(1)}, f32[128,128]{1,0:T(8,128)}, u32[]{:S(2)}) copy-start(f32[128,128]{1,0:T(8,128)} %fusion.217) | copy-start | bytes 196612
  71.0 0.7 copy-start.14
  84.6 0.7 copy-start.17
  85.6 1.2 copy-start.12
  85.8 1.0 copy-start.13
  86.8 153.4 %all-gather.16.cloned.1.call-start = ((), (), s32[]{:S(2)}) async-start(), calls=%async_computation.2 | async-start | bytes 1179648 | tf_op jit(solution)/shard_map/all_gather | solution.py:30
  86.9 38.1 %copy-start.15 = (f32[16,16,128]{2,1,0:T(8,128)S(1)}, f32[16,16,128]{2,1,0:T(8,128)}, u32[]{:S(2)}) copy-start(f32[16,16,128]{2,1,0:T(8,128)} %copy-done.14) | copy-start | bytes 393220
  146.0 64.2 %copy-start = (f32[16,16,128]{2,1,0:T(8,128)}, f32[16,16,128]{2,1,0:T(8,128)S(1)}, u32[]{:S(2)}) copy-start(f32[16,16,128]{2,1,0:T(8,128)S(1)} %fusion.45) | copy-start | bytes 393220
  146.3 1.2 copy-start.24
  147.0 1.2 copy-start.26
  147.4 1.3 copy-start.9
  147.7 1.2 copy-start.28
  148.4 1.2 copy-start.30
  151.3 5.9 %collective-permute-start.1 = (f32[1,16,16,128]{3,2,1,0:T(8,128)S(1)}, f32[1,16,16,128]{3,2,1,0:T(8,128)S(1)}, u32[]{:S(2)}, u32[]{:S(2)}) collective-permute-start(f32[1,16,16,128]{3,2,1,0:T(8,128)S(1)} %fusion.8), channel_id=1, source_target_pairs={{2,0},{4,2},{6,4},{8,6},{10,8},{12,10},{14,12},{16,14},{18,16},{20... | collective-permute-start | bytes 393224 | tf_op jit(solution)/shard_map/ppermute | solution.py:16
  158.8 11.9 %copy-start.5 = (f32[512,128]{1,0:T(8,128)S(1)}, f32[512,128]{1,0:T(8,128)}, u32[]{:S(2)}) copy-start(f32[512,128]{1,0:T(8,128)} %copy-done.4) | copy-start | bytes 786436
  160.0 10.6 %copy-start.22 = (f32[1,16,16,128]{3,2,1,0:T(8,128)}, f32[1,16,16,128]{3,2,1,0:T(8,128)S(1)}, u32[]{:S(2)}) copy-start(f32[1,16,16,128]{3,2,1,0:T(8,128)S(1)} %fusion.89) | copy-start | bytes 393220
  170.6 17.1 %copy-start.33 = (f32[128,128]{1,0:T(8,128)S(1)}, f32[128,128]{1,0:T(8,128)}, u32[]{:S(2)}) copy-start(f32[128,128]{1,0:T(8,128)} %copy-done.32) | copy-start | bytes 196612
  170.6 17.1 %copy-start.35 = (f32[128,128]{1,0:T(8,128)S(1)}, f32[128,128]{1,0:T(8,128)}, u32[]{:S(2)}) copy-start(f32[128,128]{1,0:T(8,128)} %copy-done.34) | copy-start | bytes 196612
  171.4 38.8 %copy-start.11 = (bf16[1,1,128,128]{2,3,1,0:T(8,128)(2,1)S(1)}, bf16[1,1,128,128]{2,3,1,0:T(8,128)(2,1)}, u32[]{:S(2)}) copy-start(bf16[1,1,128,128]{2,3,1,0:T(8,128)(2,1)} %copy-done.10) | copy-start | bytes 98308
  184.0 0.7 copy-start.18
  186.2 25.9 %copy-start.16 = (f32[16,16,128]{2,1,0:T(8,128)S(1)}, f32[16,16,128]{2,1,0:T(8,128)}, u32[]{:S(2)}) copy-start(f32[16,16,128]{2,1,0:T(8,128)} %convolution_add_fusion.21) | copy-start | bytes 393220
  186.2 25.9 %copy-start.19 = (f32[16,16,128]{2,1,0:T(8,128)S(1)}, f32[16,16,128]{2,1,0:T(8,128)}, u32[]{:S(2)}) copy-start(f32[16,16,128]{2,1,0:T(8,128)} %copy-done.18) | copy-start | bytes 393220
  213.3 36.5 %copy-start.42 = (f32[16,16,128]{2,1,0:T(8,128)S(1)}, f32[16,16,128]{2,1,0:T(8,128)}, u32[]{:S(2)}) copy-start(f32[16,16,128]{2,1,0:T(8,128)} %convolution_add_fusion.12) | copy-start | bytes 393220
  241.4 8.6 %copy-start.23 = (f32[1,16,16,128]{3,2,1,0:T(8,128)S(1)}, f32[1,16,16,128]{3,2,1,0:T(8,128)}, u32[]{:S(2)}) copy-start(f32[1,16,16,128]{3,2,1,0:T(8,128)} %copy-done.22) | copy-start | bytes 393220
  242.6 8.4 %copy-start.31 = (bf16[1,16,16,1152]{3,2,1,0:T(8,128)(2,1)S(1)}, bf16[1,16,16,1152]{3,2,1,0:T(8,128)(2,1)}, u32[]{:S(2)}) copy-start(bf16[1,16,16,1152]{3,2,1,0:T(8,128)(2,1)} %copy-done.30) | copy-start | bytes 1769476
  250.0 1.6 copy-start.21
  251.0 1.1 copy-start.29
  252.1 1.1 copy-start.27
  253.1 1.1 copy-start.25
Sparse Core Ops, SparseCore 0:
  86.9 49.0 all-gather.13
  186.3 53.8 all-gather.15
where the time goes:
time: 313 us; the launch traced here: 312 us
  blocking collectives  144 us (46%)
  matrix products  48.9 us (16%)
  waiting for transfers between devices  41.5 us (13%)
  other arithmetic  27.9 us (9%)
  local copies, waits for them, and re-layouts  27.3 us (9%)
  between operations  16.1 us (5%)
  starting transfers between devices  5.96 us (2%)
    all_gather x10, blocking collectives, prefix_by_axis(): pieces = jax.tree.map(lambda part: lax.all_gather(part, axis), subtotal)  131 us
    dot_general x62, matrix products, full_dot(): jnp.dot(left, right, precision=lax.Precision.HIGHEST, preferred_element_t...  39.3 us
    all_gather x2, waiting for transfers between devices, prefix_by_axis(): pieces = jax.tree.map(lambda part: lax.all_gather(part, axis), subtotal)  37.7 us
    reduce_sum x1, other arithmetic, taken_together(): return copy_for_each(shard, axis).sum(axis=0)  23.1 us
    all_to_all x1, blocking collectives, copy_for_each(): lax.all_to_all(jnp.broadcast_to(shard[None], (peers, *shard.shape)), axis...  13.7 us
    broadcast_in_dim x1, local copies, waits for them, and re-layouts, copy_for_each(): jnp.broadcast_to(shard[None], (peers, *shard.shape))  11.2 us
    unnamed x266, local copies, waits for them, and re-layouts  9.66 us
    dot_general x23, matrix products, convolve(): jnp.dot(patches(image), weights_flat, preferred_element_type=jnp.float32)  8.1 us
  transfers between devices with their start and end apart: 4, of which 3 were waited for; matrix products, arithmetic and copies ran while one was open for 6% of the time, Pallas kernels for 0%

commit v1 on v0

v1 whole, which is shorter than its diff:
```python
import functools

import jax
import jax.numpy as jnp
from jax import lax
from jax.experimental import pallas as pl
from jax.experimental.pallas import tpu as pltpu
from jax.sharding import Mesh
from jax.sharding import PartitionSpec as P

LAYER = ("layer_0", "layer_1", "layer_2")
AXES = LAYER + ("batch",)
MESH = pl.DeviceIdType.MESH
STEP = 0.1
F32 = jnp.float32
BF16 = jnp.bfloat16


def split(value):
    high = value.astype(BF16)
    return high, (value - high.astype(F32)).astype(BF16)


def dot(left, right, flip=False):
    contract = (((1,), (1,)), ((), ())) if flip else (((1,), (0,)), ((), ()))
    return lax.dot_general(left, right, contract, preferred_element_type=F32)


def times_exact(left, exact, flip=False):
    high, low = split(left)
    return dot(high, exact, flip) + dot(low, exact, flip)


def exact_times(exact, right):
    high, low = split(right)
    return dot(exact, high) + dot(exact, low)


def times(left, right, flip=False):
    high, low = split(left)
    right_high, right_low = split(right)
    return dot(high, right_high, flip) + (dot(low, right_high, flip) + dot(high, right_low, flip))


def kernel(
    sizes, blocks, side, batch,
    k_hbm, b_hbm, st_hbm, ad_hbm,
    ns_out, ne_out, na_out, nb_out, gk_out, gb_out,
    w, bias, states, guess,
    xs, xt, slopes,
    kx, ry, pz, pm, sm, pr, sr,
    shift_src, shift_dst, c_buf, v_src, v_dst,
    w_src, up, tz, row_src, down, results, lam_ref,
    g_own, g_got, gb_own, gb_got,
    in_sem, out_sem,
    mat_s, mat_r, pair_s, pair_r,
    shift_s, shift_r, chain_s, chain_r,
    up_s, up_r, z_s, z_r, down_s, down_r,
    g_s, g_r, gb_s, gb_r,
):
    nz, ny, nx, nb = sizes
    plane = ny * nx
    ch = w.shape[-1]
    cells = side * side
    own_cells = cells // plane
    coarse_step = blocks * STEP
    z, y, x = (lax.axis_index(a) for a in LAYER)
    b = lax.axis_index("batch")
    me = y * nx + x
    pos = z * plane + me
    last = nz * plane - 1
    first = pos == 0
    final = pos == last

    def device(position):
        return (position // plane, lax.rem(position // nx, ny), lax.rem(position, nx), b)

    ahead = device(lax.rem(pos + 1, last + 1))
    behind = device(lax.rem(pos + last, last + 1))
    partner = (z, y, x, 1 - b)

    def mate(k):
        t = lax.rem(me + k, plane)
        return t, (z, t // nx, lax.rem(t, nx), b)

    def copy(src, dst, send, recv, to):
        return pltpu.make_async_remote_copy(
            src_ref=src, dst_ref=dst, send_sem=send, recv_sem=recv, device_id=to, device_id_type=MESH
        )

    loads = [
        pltpu.make_async_copy(st_hbm, states, in_sem.at[0]),
        pltpu.make_async_copy(b_hbm, bias, in_sem.at[1]),
        pltpu.make_async_copy(ad_hbm, guess, in_sem.at[2]),
    ] + [pltpu.make_async_copy(k_hbm.at[n], w.at[n], in_sem.at[3 + n]) for n in range(blocks)]
    for c in loads:
        c.start()

    barrier = pltpu.get_barrier_semaphore()

    def greet(to):
        pl.semaphore_signal(barrier, inc=1, device_id=to, device_id_type=MESH)

    greet(ahead)
    greet(behind)
    greet(partner)
    for k in range(1, plane):
        greet(mate(k)[1])
    for k in range(1, nz):
        greet((lax.rem(z + k, nz), y, x, b))
    greeted = 3 + plane - 1 + nz - 1

    for d in range(3):
        xs[d, 0:side, :] = jnp.zeros((side, ch), BF16)
        xs[d, side + cells : 2 * side + cells, :] = jnp.zeros((side, ch), BF16)
    column = lax.rem(lax.broadcasted_iota(jnp.int32, (cells, ch), 0), side)
    inner_left = column != 0
    inner_right = column != side - 1
    for c in loads:
        c.wait()

    def place(value):
        xs[1, side : side + cells, :] = value.astype(BF16)
        xs[0, side : side + cells, :] = jnp.where(inner_left, pltpu.roll(value, 1, 0), 0.0).astype(BF16)
        xs[2, side : side + cells, :] = jnp.where(inner_right, pltpu.roll(value, cells - 1, 0), 0.0).astype(BF16)

    def patches():
        return jnp.concatenate(
            [xs[dx, side * dy : side * dy + cells, :] for dy in range(3) for dx in range(3)], axis=1
        )

    def activate(n, u):
        place(u)
        return jnp.tanh(dot(patches(), w[n]) + bias[pl.ds(n, 1), :])

    def adjoint_conv(n, columns):
        flipped = jnp.concatenate([w[n, ch * (8 - t) : ch * (9 - t), :] for t in range(9)], axis=1)
        return dot(columns, flipped, True)

    def relax(u):
        return lax.fori_loop(0, blocks, lambda n, s: s + STEP * activate(n, s), u)

    def back_relax(lam):
        def body(k, lam):
            n = blocks - 1 - k
            place(slopes[n] * lam)
            return lam + STEP * adjoint_conv(n, patches())

        return lax.fori_loop(0, blocks, body, lam)

    eye = (
        lax.broadcasted_iota(jnp.int32, (ch, ch), 0) == lax.broadcasted_iota(jnp.int32, (ch, ch), 1)
    ).astype(F32)
    centre = w[0, 4 * ch : 5 * ch, :]
    half = ch // nb
    mine = pl.ds(pl.multiple_of(half * b, half), half)
    other = pl.ds(pl.multiple_of(half * (1 - b), half), half)

    def mats(level, buf, index, size, to):
        def start():
            for k in range(1, size):
                copy(
                    buf.at[index, mine], buf.at[index, mine], mat_s.at[level, k], mat_r.at[level, k],
                    to(lax.rem(index + k, size)),
                ).start()

        def relay():
            for k in range(1, size):
                source = lax.rem(index - k + size, size)
                copy(
                    buf.at[source, mine], buf.at[source, mine], mat_s.at[level, k], mat_r.at[level, k], partner
                ).wait_recv()
                copy(
                    buf.at[source, mine], buf.at[source, mine], pair_s.at[level, k], pair_r.at[level, k], partner
                ).start()

        def finish():
            for k in range(1, size):
                source = lax.rem(index - k + size, size)
                copy(
                    buf.at[source, other], buf.at[source, other], pair_s.at[level, k], pair_r.at[level, k], partner
                ).wait_recv()

        def drain():
            for k in range(1, size):
                source = lax.rem(index - k + size, size)
                copy(
                    buf.at[index, mine], buf.at[index, mine], mat_s.at[level, k], mat_r.at[level, k], partner
                ).wait_send()
                copy(
                    buf.at[source, mine], buf.at[source, mine], pair_s.at[level, k], pair_r.at[level, k], partner
                ).wait_send()

        return start, relay, finish, drain

    row_mats = mats(0, kx, x, nx, lambda t: (z, y, t, b))
    column_mats = mats(1, ry, y, ny, lambda t: (z, t, x, b))
    z_mats = mats(2, pz, z, nz, lambda t: (t, y, x, b))

    kx[x] = centre.astype(F32)
    relaxed = relax(states[...])
    pl.semaphore_wait(barrier, greeted)
    row_mats[0]()
    shift_src[0] = relaxed
    forward_shift = copy(shift_src.at[0], shift_dst.at[0], shift_s.at[0], shift_r.at[0], ahead)
    forward_shift.start()

    row_mats[1]()
    row_mats[2]()
    pm[0] = eye
    for j in range(nx):
        pm[j + 1] = pm[j] + coarse_step * times_exact(pm[j], kx[j].astype(BF16))
    sm[nx - 1] = eye
    for j in range(nx - 1, 0, -1):
        sm[j - 1] = sm[j] + coarse_step * exact_times(kx[j].astype(BF16), sm[j])
    ry[y] = pm[nx]
    column_mats[0]()

    def coarse_of(field, flip):
        return field + coarse_step * times_exact(field, centre, flip)

    def scan(d, extra_up, extra_z):
        flip = d == 1
        row_later, row_sooner = (pm, sm) if flip else (sm, pm)
        column_later, column_sooner = (pr, sr) if flip else (sr, pr)
        w_src[d] = times(c_buf[d], row_later[x], flip)
        for k in range(1, plane):
            t, to = mate(k)
            piece = pl.ds(pl.multiple_of(own_cells * t, own_cells), own_cells)
            copy(w_src.at[d, piece], up.at[d, me], up_s.at[d, k], up_r.at[d, k], to).start()
        own = pl.ds(pl.multiple_of(own_cells * me, own_cells), own_cells)
        up[d, me] = w_src[d, own]

        def chain_copy():
            to = lax.rem(x + (nx - 1 if flip else 1), nx)
            return copy(v_src.at[d], v_dst.at[d], chain_s.at[d], chain_r.at[d], (z, y, to, b))

        def chain(k):
            sender = nx - 1 - k if flip else k
            if k >= nx - 1:
                return

            @pl.when(x == sender)
            def _():
                if k == 0:
                    v_src[d] = c_buf[d]
                else:
                    chain_copy().wait_recv()
                    v_src[d] = coarse_of(v_dst[d], flip) + c_buf[d]
                chain_copy().start()

        chain(0)
        extra_up()
        for k in range(1, plane):
            source = lax.rem(me - k + plane, plane)
            copy(w_src.at[d, own], up.at[d, source], up_s.at[d, k], up_r.at[d, k], partner).wait_recv()
        row_total = [sum(up[d, r * nx + i] for i in range(nx)) for r in range(ny)]
        tz[d, z] = sum(times(row_total[r], column_later[r], flip) for r in range(ny))
        for k in range(1, nz):
            to = lax.rem(z + k, nz)
            copy(tz.at[d, z], tz.at[d, z], z_s.at[d, k], z_r.at[d, k], (to, y, x, b)).start()
        inside = [None] * ny
        order = list(range(ny - 1, -1, -1)) if flip else list(range(ny))
        inside[order[0]] = jnp.zeros((own_cells, ch), F32)
        for r, s in zip(order, order[1:]):
            inside[s] = times(inside[r], ry[r], flip) + row_total[r]
        chain(1)
        extra_z()
        for k in range(1, nz):
            source = lax.rem(z - k + nz, nz)
            copy(tz.at[d, source], tz.at[d, source], z_s.at[d, k], z_r.at[d, k], partner).wait_recv()

        def advance(k, s):
            i = nz - 1 - k if flip else k
            return times(s, pz[i], flip) + tz[d, i]

        entering = lax.fori_loop(0, nz - 1 - z if flip else z, advance, jnp.zeros((own_cells, ch), F32))
        for r in range(ny):
            row_src[d, r] = times(entering, column_sooner[r], flip) + inside[r]
        for k in range(1, plane):
            t, to = mate(k)
            copy(row_src.at[d, t // nx], down.at[d, own], down_s.at[d, k], down_r.at[d, k], to).start()
        down[d, own] = row_src[d, y]
        for k in range(2, nx - 1):
            chain(k)
        for k in range(1, plane):
            source = lax.rem(me - k + plane, plane)
            piece = pl.ds(pl.multiple_of(own_cells * source, own_cells), own_cells)
            copy(row_src.at[d, y], down.at[d, piece], down_s.at[d, k], down_r.at[d, k], partner).wait_recv()
        results[d] = times(down[d], row_sooner[x], flip)

        @pl.when(x == (0 if flip else nx - 1))
        def _():
            chain_copy().wait_recv()

        @pl.when(x != (nx - 1 if flip else 0))
        def _():
            results[d] = results[d] + v_dst[d]

        def drain():
            for k in range(1, plane):
                copy(w_src.at[d, own], up.at[d, me], up_s.at[d, k], up_r.at[d, k], partner).wait_send()
                copy(row_src.at[d, y], down.at[d, own], down_s.at[d, k], down_r.at[d, k], partner).wait_send()
            for k in range(1, nz):
                copy(tz.at[d, z], tz.at[d, z], z_s.at[d, k], z_r.at[d, k], partner).wait_send()

            @pl.when(x != (0 if flip else nx - 1))
            def _():
                chain_copy().wait_send()

        return drain

    forward_shift.wait_recv()
    start = jnp.where(first, states[...], shift_dst[0])
    c_buf[0] = jnp.where(first, 0.0, -coarse_of(start, False)) + relax(start)

    def extra_up():
        column_mats[1]()
        column_mats[2]()
        pr[0] = eye
        for j in range(ny):
            pr[j + 1] = times(pr[j], ry[j])
        sr[ny - 1] = eye
        for j in range(ny - 1, 0, -1):
            sr[j - 1] = times(ry[j], sr[j])
        pz[z] = pr[ny]
        z_mats[0]()

    def extra_z():
        z_mats[1]()
        z_mats[2]()

    forward_drain = scan(0, extra_up, extra_z)
    results[0] = jnp.where(first, states[...], results[0])
    outs = [pltpu.make_async_copy(results.at[0], ns_out, out_sem.at[0])]
    outs[0].start()

    def final_step(n, u):
        activ = activate(n, u)
        xt[n] = jnp.transpose(xs[1, side : side + cells, :].astype(F32)).astype(BF16)
        slopes[n] = 1.0 - activ * activ
        return u + STEP * activ

    lax.fori_loop(0, blocks, final_step, results[0])

    shift_src[1] = back_relax(guess[...])
    back_shift = copy(shift_src.at[1], shift_dst.at[1], shift_s.at[1], shift_r.at[1], behind)
    back_shift.start()
    new_ends = jnp.where(first, 0.0, coarse_of(results[0], False)) + c_buf[0]
    v_src[2] = new_ends
    outs.append(pltpu.make_async_copy(v_src.at[2], ne_out, out_sem.at[1]))
    outs[-1].start()
    back_shift.wait_recv()
    back_start = jnp.where(final, guess[...], shift_dst[1])
    c_buf[1] = jnp.where(final, 0.0, -coarse_of(back_start, True)) + back_relax(back_start)
    back_drain = scan(1, lambda: None, lambda: None)
    results[1] = jnp.where(final, guess[...], results[1])
    outs.append(pltpu.make_async_copy(results.at[1], na_out, out_sem.at[2]))
    outs[-1].start()

    def grad_copy(n):
        return copy(g_own.at[n], g_got.at[n], g_s.at[n], g_r.at[n], partner)

    lam_ref[...] = results[1]
    for n in range(blocks - 1, -1, -1):
        sens = slopes[n] * lam_ref[...]
        place(sens)
        columns = patches()
        if n > 0:
            lam_ref[...] = lam_ref[...] + STEP * adjoint_conv(n, columns)
        gb_own[n : n + 1, :] = jnp.sum(sens.astype(BF16).astype(F32), axis=0, keepdims=True)
        product = dot(xt[n], columns)
        for t in range(9):
            g_own[n, t] = product[:, ch * (8 - t) : ch * (9 - t)]
        grad_copy(n).start()
    bias_copy = copy(gb_own, gb_got, gb_s, gb_r, partner)
    bias_copy.start()
    new_back = jnp.where(final, 0.0, coarse_of(results[1], True)) + c_buf[1]
    v_src[3] = new_back
    outs.append(pltpu.make_async_copy(v_src.at[3], nb_out, out_sem.at[3]))
    outs[-1].start()
    factor = STEP / (nb * batch * cells)
    for n in range(blocks - 1, -1, -1):
        grad_copy(n).wait_recv()
        g_got[n] = factor * (g_own[n] + g_got[n])
        outs.append(pltpu.make_async_copy(g_got.at[n], gk_out.at[n], out_sem.at[4 + n]))
        outs[-1].start()
    bias_copy.wait_recv()
    gb_got[...] = factor * (gb_own[...] + gb_got[...])
    outs.append(pltpu.make_async_copy(gb_got, gb_out, out_sem.at[4 + blocks]))
    outs[-1].start()

    for n in range(blocks):
        grad_copy(n).wait_send()
    bias_copy.wait_send()
    forward_shift.wait_send()
    back_shift.wait_send()
    row_mats[3]()
    column_mats[3]()
    z_mats[3]()
    forward_drain()
    back_drain()
    for c in outs:
        c.wait()


def body(sizes, kernels, biases, states, adjoint_guess):
    nz, ny, nx, nb = sizes
    plane = ny * nx
    blocks, taps, ch, _ = kernels.shape
    side = states.shape[2]
    batch = states.shape[1]
    cells = side * side
    own = cells // plane
    field = jax.ShapeDtypeStruct((cells, ch), F32)
    dma = pltpu.SemaphoreType.DMA
    most = max(nz, ny, nx)
    vmem = pltpu.VMEM
    scratch = [
        vmem((blocks, taps * ch, ch), BF16),
        vmem((blocks, ch), F32),
        vmem((cells, ch), F32),
        vmem((cells, ch), F32),
        vmem((3, cells + 2 * side, ch), BF16),
        vmem((blocks, ch, cells), BF16),
        vmem((blocks, cells, ch), F32),
        vmem((nx, ch, ch), F32),
        vmem((ny, ch, ch), F32),
        vmem((nz, ch, ch), F32),
        vmem((nx + 1, ch, ch), F32),
        vmem((nx, ch, ch), F32),
        vmem((ny + 1, ch, ch), F32),
        vmem((ny, ch, ch), F32),
        vmem((2, cells, ch), F32),
        vmem((2, cells, ch), F32),
        vmem((2, cells, ch), F32),
        vmem((4, cells, ch), F32),
        vmem((2, cells, ch), F32),
        vmem((2, cells, ch), F32),
        vmem((2, plane, own, ch), F32),
        vmem((2, nz, own, ch), F32),
        vmem((2, ny, own, ch), F32),
        vmem((2, cells, ch), F32),
        vmem((2, cells, ch), F32),
        vmem((cells, ch), F32),
        vmem((blocks, taps, ch, ch), F32),
        vmem((blocks, taps, ch, ch), F32),
        vmem((blocks, ch), F32),
        vmem((blocks, ch), F32),
        dma((3 + blocks,)),
        dma((5 + blocks,)),
        dma((3, most)),
        dma((3, most)),
        dma((3, most)),
        dma((3, most)),
        dma((2,)),
        dma((2,)),
        dma((2,)),
        dma((2,)),
        dma((2, plane)),
        dma((2, plane)),
        dma((2, nz)),
        dma((2, nz)),
        dma((2, plane)),
        dma((2, plane)),
        dma((blocks,)),
        dma((blocks,)),
        dma(()),
        dma(()),
    ]
    any_space = pl.BlockSpec(memory_space=pl.ANY)
    outs = pl.pallas_call(
        functools.partial(kernel, sizes, blocks, side, batch),
        out_shape=[field] * 4
        + [jax.ShapeDtypeStruct((blocks, taps, ch, ch), F32), jax.ShapeDtypeStruct((blocks, ch), F32)],
        in_specs=[any_space] * 4,
        out_specs=[any_space] * 6,
        scratch_shapes=scratch,
        compiler_params=pltpu.CompilerParams(
            collective_id=0, has_side_effects=True, vmem_limit_bytes=40 * 1024 * 1024
        ),
        name="vcycle",
    )(
        kernels.reshape(blocks, taps * ch, ch),
        biases,
        states.reshape(cells, ch),
        adjoint_guess.reshape(cells, ch),
    )
    fields = [out.reshape(states.shape) for out in outs[:4]]
    return (*fields, outs[4], outs[5])


def solution(mesh, sizes=(8, 4, 4)):
    sizes = (*sizes, mesh.shape["batch"])
    torus = Mesh(mesh.devices.reshape(sizes), AXES)
    state = P(LAYER, "batch", None, None, None)
    return jax.shard_map(
        functools.partial(body, sizes),
        mesh=torus,
        in_specs=(P(LAYER, None, None, None), P(LAYER, None), state, state),
        out_specs=(state, state, state, state, P(LAYER, None, None, None), P(LAYER, None)),
        check_vma=False,
    )
```

time: 313 us -> 86.3 us (0.28)
  blocking collectives: 144 us -> 0 us
  Pallas kernels: 0 us -> 77.1 us
  matrix products: 48.9 us -> 0 us
  waiting for transfers between devices: 41.5 us -> 0 us
  other arithmetic: 27.9 us -> 0 us
  local copies, waits for them, and re-layouts: 27.3 us -> 8.36 us
  between operations: 16.1 us -> 0.65 us
  starting transfers between devices: 5.96 us -> 0 us
    all_gather x10 -> x0, blocking collectives: 131 us -> none  [prefix_by_axis(): pieces = jax.tree.map(lambda part: lax.all_gather(part, axis), subtotal)]
    pallas_call x0 -> x1, Pallas kernels: none -> 77.1 us  [body(): pl.pallas_call(functools.partial(kernel, sizes, blocks, side, batch), out...]
    dot_general x89 -> x0, matrix products: 48.9 us -> none  [the longest x62 39.3 us: full_dot(): jnp.dot(left, right, precision=lax.Precision.HIGHEST, preferred_element_t...]
    all_gather x2 -> x0, waiting for transfers between devices: 37.7 us -> none  [prefix_by_axis(): pieces = jax.tree.map(lambda part: lax.all_gather(part, axis), subtotal)]
    reduce_sum x1 -> x0, other arithmetic: 23.1 us -> none  [taken_together(): return copy_for_each(shard, axis).sum(axis=0)]
    all_to_all x1 -> x0, blocking collectives: 13.7 us -> none  [copy_for_each(): lax.all_to_all(jnp.broadcast_to(shard[None], (peers, *shard.shape)), axis...]
    broadcast_in_dim x1 -> x0, local copies, waits for them, and re-layouts: 11.2 us -> none  [copy_for_each(): jnp.broadcast_to(shard[None], (peers, *shard.shape))]
    ppermute x2 -> x0, starting transfers between devices: 5.88 us -> none  [from_behind(): lax.ppermute(value, axis, [(source, source + steps) for source in range(l...]
  transfers between devices with their start and end apart: 4 -> 0, of which waited for: 3 -> 0; matrix products, arithmetic and copies ran while one was open for 6% -> 0% of each run, Pallas kernels for 0% -> 0%
where the time goes in v1:
time: 86.3 us; the launch traced here: 86.2 us
  Pallas kernels  77.1 us (89%)
  local copies, waits for them, and re-layouts  8.36 us (10%)
    pallas_call x1, Pallas kernels, body(): pl.pallas_call(functools.partial(kernel, sizes, blocks, side, batch), out...  77.1 us
    unnamed x14, local copies, waits for them, and re-layouts  8.36 us

profile of v1, /device:TPU:1, one launch (start us, length us, event | category | flops | bytes accessed | tf_op | source)
XLA Modules:
  0.0 86.2 jit_solution(9367115337877290726)
XLA Ops:
  0.6 0.0 copy-start
  0.6 1.3 %copy-done = bf16[4,9,128,128]{3,2,1,0:T(8,128)(2,1)S(1)} copy-done((bf16[4,9,128,128]{3,2,1,0:T(8,128)(2,1)S(1)}, bf16[4,9,128,128]{3,2,1,0:T(8,128)(2,1)}, u32[]{:S(2)}) %copy-start) | copy-done | bytes 1179672
  1.9 0.0 copy-start.1
  1.9 0.9 %copy-done.1 = f32[1,1,16,16,128]{4,3,2,1,0:T(8,128)S(1)} copy-done((f32[1,1,16,16,128]{4,3,2,1,0:T(8,128)S(1)}, f32[1,1,16,16,128]{4,3,2,1,0:T(8,128)}, u32[]{:S(2)}) %copy-start.1) | copy-done | bytes 131096
  2.8 0.0 copy-start.2
  2.8 0.9 %copy-done.2 = f32[1,1,16,16,128]{4,3,2,1,0:T(8,128)S(1)} copy-done((f32[1,1,16,16,128]{4,3,2,1,0:T(8,128)S(1)}, f32[1,1,16,16,128]{4,3,2,1,0:T(8,128)}, u32[]{:S(2)}) %copy-start.2) | copy-done | bytes 131096
  3.7 0.0 copy-start.3
  3.7 0.7 copy-done.3
  4.4 77.1 %vcycle.1 = (f32[256,128]{1,0:T(8,128)S(1)}, f32[256,128]{1,0:T(8,128)S(1)}, f32[256,128]{1,0:T(8,128)S(1)}, f32[256,128]{1,0:T(8,128)S(1)}, f32[4,9,128,128]{3,2,1,0:T(8,128)S(1)}, /*index=5*/f32[4,128]{1,0:T(4,128)S(1)}) custom-call(bf16[4,1152,128]{2,1,0:T(8,128)(2,1)S(1)} %bitcast.7, f32[4,128]{1,0:T(4,128)S(1)} %copy-done.3, f32[256,128]{1,0:T(8,128)S(1)} %bitcast.12, ...), custom_call_target="tpu_custom_call" | custom-call | tf_op jit(solution)/shard_map/vcycle/pallas_call | solution.py:472
  81.6 0.7 copy.16
  82.2 0.7 copy.17
  82.9 0.7 copy.18
  83.5 0.7 copy.19
  84.2 1.4 %copy.20 = f32[4,9,128,128]{3,2,1,0:T(8,128)} copy(f32[4,9,128,128]{3,2,1,0:T(8,128)S(1)} %get-tuple-element.28) | data formatting | bytes 4718592
  85.6 0.6 copy.21
Async XLA Ops:
  0.6 1.3 %copy-start = (bf16[4,9,128,128]{3,2,1,0:T(8,128)(2,1)S(1)}, bf16[4,9,128,128]{3,2,1,0:T(8,128)(2,1)}, u32[]{:S(2)}) copy-start(bf16[4,9,128,128]{3,2,1,0:T(8,128)(2,1)} %param.4) | copy-start | bytes 3538948
  1.9 0.9 %copy-start.1 = (f32[1,1,16,16,128]{4,3,2,1,0:T(8,128)S(1)}, f32[1,1,16,16,128]{4,3,2,1,0:T(8,128)}, u32[]{:S(2)}) copy-start(f32[1,1,16,16,128]{4,3,2,1,0:T(8,128)} %param.6) | copy-start | bytes 393220
  2.8 0.9 %copy-start.2 = (f32[1,1,16,16,128]{4,3,2,1,0:T(8,128)S(1)}, f32[1,1,16,16,128]{4,3,2,1,0:T(8,128)}, u32[]{:S(2)}) copy-start(f32[1,1,16,16,128]{4,3,2,1,0:T(8,128)} %param.7) | copy-start | bytes 393220
  3.7 0.7 copy-start.3

commit v2 on v1

--- a/solution.py
+++ b/solution.py
@@ -51,12 +51,12 @@
     kx, ry, pz, pm, sm, pr, sr,
     shift_src, shift_dst, c_buf, v_src, v_dst,
     w_src, up, tz, row_src, down, results, lam_ref,
-    g_own, g_got, gb_own, gb_got,
+    u_own, u_got, xt_got, sens_own, sens_got, g_own, g_sum, gb_sum,
     in_sem, out_sem,
     mat_s, mat_r, pair_s, pair_r,
     shift_s, shift_r, chain_s, chain_r,
     up_s, up_r, z_s, z_r, down_s, down_r,
-    g_s, g_r, gb_s, gb_r,
+    u_s, u_r, sens_s, sens_r,
 ):
     nz, ny, nx, nb = sizes
     plane = ny * nx
@@ -198,9 +198,9 @@
     z_mats = mats(2, pz, z, nz, lambda t: (t, y, x, b))
 
     kx[x] = centre.astype(F32)
-    relaxed = relax(states[...])
     pl.semaphore_wait(barrier, greeted)
     row_mats[0]()
+    relaxed = relax(states[...])
     shift_src[0] = relaxed
     forward_shift = copy(shift_src.at[0], shift_dst.at[0], shift_s.at[0], shift_r.at[0], ahead)
     forward_shift.start()
@@ -336,12 +336,14 @@
     outs[0].start()
 
     def final_step(n, u):
+        u_own[n] = u
         activ = activate(n, u)
-        xt[n] = jnp.transpose(xs[1, side : side + cells, :].astype(F32)).astype(BF16)
         slopes[n] = 1.0 - activ * activ
         return u + STEP * activ
 
     lax.fori_loop(0, blocks, final_step, results[0])
+    inputs_copy = copy(u_own, u_got, u_s, u_r, partner)
+    inputs_copy.start()
 
     shift_src[1] = back_relax(guess[...])
     back_shift = copy(shift_src.at[1], shift_dst.at[1], shift_s.at[1], shift_r.at[1], behind)
@@ -350,6 +352,11 @@
     v_src[2] = new_ends
     outs.append(pltpu.make_async_copy(v_src.at[2], ne_out, out_sem.at[1]))
     outs[-1].start()
+    for n in range(blocks):
+        xt[n] = jnp.transpose(u_own[n]).astype(BF16)
+    inputs_copy.wait_recv()
+    for n in range(blocks):
+        xt_got[n] = jnp.transpose(u_got[n]).astype(BF16)
     back_shift.wait_recv()
     back_start = jnp.where(final, guess[...], shift_dst[1])
     c_buf[1] = jnp.where(final, 0.0, -coarse_of(back_start, True)) + back_relax(back_start)
@@ -358,41 +365,43 @@
     outs.append(pltpu.make_async_copy(results.at[1], na_out, out_sem.at[2]))
     outs[-1].start()
 
-    def grad_copy(n):
-        return copy(g_own.at[n], g_got.at[n], g_s.at[n], g_r.at[n], partner)
+    def sens_copy(n):
+        return copy(sens_own.at[n], sens_got.at[n], sens_s.at[n], sens_r.at[n], partner)
+
+    def bias_sum(sens):
+        return jnp.sum(sens.astype(BF16).astype(F32), axis=0, keepdims=True)
 
     lam_ref[...] = results[1]
     for n in range(blocks - 1, -1, -1):
         sens = slopes[n] * lam_ref[...]
+        sens_own[n] = sens
+        sens_copy(n).start()
         place(sens)
         columns = patches()
         if n > 0:
             lam_ref[...] = lam_ref[...] + STEP * adjoint_conv(n, columns)
-        gb_own[n : n + 1, :] = jnp.sum(sens.astype(BF16).astype(F32), axis=0, keepdims=True)
-        product = dot(xt[n], columns)
-        for t in range(9):
-            g_own[n, t] = product[:, ch * (8 - t) : ch * (9 - t)]
-        grad_copy(n).start()
-    bias_copy = copy(gb_own, gb_got, gb_s, gb_r, partner)
-    bias_copy.start()
+        gb_sum[n : n + 1, :] = bias_sum(sens)
+        g_own[n] = dot(xt[n], columns)
     new_back = jnp.where(final, 0.0, coarse_of(results[1], True)) + c_buf[1]
     v_src[3] = new_back
     outs.append(pltpu.make_async_copy(v_src.at[3], nb_out, out_sem.at[3]))
     outs[-1].start()
     factor = STEP / (nb * batch * cells)
     for n in range(blocks - 1, -1, -1):
-        grad_copy(n).wait_recv()
-        g_got[n] = factor * (g_own[n] + g_got[n])
-        outs.append(pltpu.make_async_copy(g_got.at[n], gk_out.at[n], out_sem.at[4 + n]))
+        sens_copy(n).wait_recv()
+        place(sens_got[n])
+        gb_sum[n : n + 1, :] = factor * (gb_sum[n : n + 1, :] + bias_sum(sens_got[n]))
+        total = factor * (g_own[n] + dot(xt_got[n], patches()))
+        for t in range(9):
+            g_sum[n, t] = total[:, ch * (8 - t) : ch * (9 - t)]
+        outs.append(pltpu.make_async_copy(g_sum.at[n], gk_out.at[n], out_sem.at[4 + n]))
         outs[-1].start()
-    bias_copy.wait_recv()
-    gb_got[...] = factor * (gb_own[...] + gb_got[...])
-    outs.append(pltpu.make_async_copy(gb_got, gb_out, out_sem.at[4 + blocks]))
+    outs.append(pltpu.make_async_copy(gb_sum, gb_out, out_sem.at[4 + blocks]))
     outs[-1].start()
 
     for n in range(blocks):
-        grad_copy(n).wait_send()
-    bias_copy.wait_send()
+        sens_copy(n).wait_send()
+    inputs_copy.wait_send()
     forward_shift.wait_send()
     back_shift.wait_send()
     row_mats[3]()
@@ -401,6 +410,15 @@
     forward_drain()
     back_drain()
     for c in outs:
+        c.wait()
+
+
+def flush(*refs):
+    sem = refs[-1]
+    copies = [pltpu.make_async_copy(refs[i], refs[6 + i], sem.at[i]) for i in range(6)]
+    for c in copies:
+        c.start()
+    for c in copies:
         c.wait()
 
 
@@ -443,9 +461,13 @@
         vmem((2, cells, ch), F32),
         vmem((2, cells, ch), F32),
         vmem((cells, ch), F32),
+        vmem((blocks, cells, ch), F32),
+        vmem((blocks, cells, ch), F32),
+        vmem((blocks, ch, cells), BF16),
+        vmem((blocks, cells, ch), F32),
+        vmem((blocks, cells, ch), F32),
+        vmem((blocks, ch, taps * ch), F32),
         vmem((blocks, taps, ch, ch), F32),
-        vmem((blocks, taps, ch, ch), F32),
-        vmem((blocks, ch), F32),
         vmem((blocks, ch), F32),
         dma((3 + blocks,)),
         dma((5 + blocks,)),
@@ -463,17 +485,17 @@
         dma((2, nz)),
         dma((2, plane)),
         dma((2, plane)),
+        dma(()),
+        dma(()),
         dma((blocks,)),
         dma((blocks,)),
-        dma(()),
-        dma(()),
     ]
     any_space = pl.BlockSpec(memory_space=pl.ANY)
     outs = pl.pallas_call(
         functools.partial(kernel, sizes, blocks, side, batch),
         out_shape=[field] * 4
         + [jax.ShapeDtypeStruct((blocks, taps, ch, ch), F32), jax.ShapeDtypeStruct((blocks, ch), F32)],
-        in_specs=[any_space] * 4,
+        in_specs=[pl.BlockSpec(memory_space=pltpu.HBM)] * 4,
         out_specs=[any_space] * 6,
         scratch_shapes=scratch,
         compiler_params=pltpu.CompilerParams(
@@ -481,11 +503,25 @@
         ),
         name="vcycle",
     )(
-        kernels.reshape(blocks, taps * ch, ch),
-        biases,
-        states.reshape(cells, ch),
-        adjoint_guess.reshape(cells, ch),
+        *(
+            pltpu.with_memory_space_constraint(a, pltpu.HBM)
+            for a in (
+                kernels.reshape(blocks, taps * ch, ch),
+                biases,
+                states.reshape(cells, ch),
+                adjoint_guess.reshape(cells, ch),
+            )
+        )
     )
+    outs = pl.pallas_call(
+        flush,
+        out_shape=[jax.ShapeDtypeStruct(out.shape, out.dtype) for out in outs],
+        in_specs=[any_space] * 6,
+        out_specs=[pl.BlockSpec(memory_space=pltpu.HBM)] * 6,
+        scratch_shapes=[dma((6,))],
+        compiler_params=pltpu.CompilerParams(vmem_limit_bytes=1024 * 1024),
+        name="flush",
+    )(*outs)
     fields = [out.reshape(states.shape) for out in outs[:4]]
     return (*fields, outs[4], outs[5])
 

time: 86.3 us -> 77.1 us (0.89)
  local copies, waits for them, and re-layouts: 8.36 us -> 0 us
    unnamed x14 -> x0, local copies, waits for them, and re-layouts: 8.36 us -> none
    pallas_call x1, Pallas kernels: 77.1 us -> 74.7 us  [body(): pl.pallas_call(functools.partial(kernel, sizes, blocks, side, batch), out...]
    pallas_call x0 -> x1, Pallas kernels: none -> 1.64 us  [body(): pl.pallas_call(flush, out_shape=[jax.ShapeDtypeStruct(out.shape, out.dtyp...]
where the time goes in v2:
time: 77.1 us; the launch traced here: 77 us
  Pallas kernels  76.4 us (99%)
    pallas_call x1, Pallas kernels, body(): pl.pallas_call(functools.partial(kernel, sizes, blocks, side, batch), out...  74.7 us
    pallas_call x1, Pallas kernels, body(): pl.pallas_call(flush, out_shape=[jax.ShapeDtypeStruct(out.shape, out.dtyp...  1.64 us

profile of v2, /device:TPU:1, one launch (start us, length us, event | category | flops | bytes accessed | tf_op | source)
XLA Modules:
  0.0 77.0 jit_solution(14803375347795258100)
XLA Ops:
  0.6 74.7 %vcycle.1 = (f32[256,128]{1,0:T(8,128)S(1)}, f32[256,128]{1,0:T(8,128)S(1)}, f32[256,128]{1,0:T(8,128)S(1)}, f32[256,128]{1,0:T(8,128)S(1)}, f32[4,9,128,128]{3,2,1,0:T(8,128)S(1)}, /*index=5*/f32[4,128]{1,0:T(4,128)S(1)}) custom-call(bf16[4,1152,128]{2,1,0:T(8,128)(2,1)} %bitcast.7, f32[4,128]{1,0:T(4,128)} %b_hbm.1, f32[256,128]{1,0:T(8,128)} %bitcast.8, ...), custom_call_target="tpu_custom_call" | custom-call | tf_op jit(solution)/shard_map/vcycle/pallas_call | solution.py:494
  75.4 1.6 %flush.1 = (f32[256,128]{1,0:T(8,128)}, f32[256,128]{1,0:T(8,128)}, f32[256,128]{1,0:T(8,128)}, f32[256,128]{1,0:T(8,128)}, f32[4,9,128,128]{3,2,1,0:T(8,128)}, /*index=5*/f32[4,128]{1,0:T(4,128)}) custom-call(f32[256,128]{1,0:T(8,128)S(1)} %get-tuple-element.18.refs_0_, f32[256,128]{1,0:T(8,128)S(1)} %get-tuple-element.19.refs_1_, ...), custom_call_target="tpu_custom_call" | custom-call | tf_op jit(solution)/shard_map/flush/pallas_call | solution.py:516

commit v3 on v2

--- a/solution.py
+++ b/solution.py
@@ -46,7 +46,7 @@
     sizes, blocks, side, batch,
     k_hbm, b_hbm, st_hbm, ad_hbm,
     ns_out, ne_out, na_out, nb_out, gk_out, gb_out,
-    w, bias, states, guess,
+    w, bias, states, guess, middle,
     xs, xt, slopes,
     kx, ry, pz, pm, sm, pr, sr,
     shift_src, shift_dst, c_buf, v_src, v_dst,
@@ -79,9 +79,18 @@
     behind = device(lax.rem(pos + last, last + 1))
     partner = (z, y, x, 1 - b)
 
-    def mate(k):
-        t = lax.rem(me + k, plane)
-        return t, (z, t // nx, lax.rem(t, nx), b)
+    def ring(step, size):
+        return min(step, size - step)
+
+    offsets = sorted(
+        ((dy, dx) for dy in range(ny) for dx in range(nx) if dy or dx),
+        key=lambda o: -ring(o[0], ny) - ring(o[1], nx),
+    )
+    z_steps = sorted(range(1, nz), key=lambda k: -ring(k, nz))
+
+    def mate(offset):
+        ty, tx = lax.rem(y + offset[0], ny), lax.rem(x + offset[1], nx)
+        return ty, ty * nx + tx, (z, ty, tx, b)
 
     def copy(src, dst, send, recv, to):
         return pltpu.make_async_remote_copy(
@@ -89,10 +98,12 @@
         )
 
     loads = [
-        pltpu.make_async_copy(st_hbm, states, in_sem.at[0]),
-        pltpu.make_async_copy(b_hbm, bias, in_sem.at[1]),
-        pltpu.make_async_copy(ad_hbm, guess, in_sem.at[2]),
-    ] + [pltpu.make_async_copy(k_hbm.at[n], w.at[n], in_sem.at[3 + n]) for n in range(blocks)]
+        pltpu.make_async_copy(k_hbm.at[0, 4 * ch : 5 * ch], middle, in_sem.at[0]),
+        pltpu.make_async_copy(st_hbm, states, in_sem.at[1]),
+        pltpu.make_async_copy(b_hbm, bias, in_sem.at[2]),
+        pltpu.make_async_copy(k_hbm, w, in_sem.at[3]),
+        pltpu.make_async_copy(ad_hbm, guess, in_sem.at[4]),
+    ]
     for c in loads:
         c.start()
 
@@ -104,8 +115,8 @@
     greet(ahead)
     greet(behind)
     greet(partner)
-    for k in range(1, plane):
-        greet(mate(k)[1])
+    for o in offsets:
+        greet(mate(o)[2])
     for k in range(1, nz):
         greet((lax.rem(z + k, nz), y, x, b))
     greeted = 3 + plane - 1 + nz - 1
@@ -116,8 +127,6 @@
     column = lax.rem(lax.broadcasted_iota(jnp.int32, (cells, ch), 0), side)
     inner_left = column != 0
     inner_right = column != side - 1
-    for c in loads:
-        c.wait()
 
     def place(value):
         xs[1, side : side + cells, :] = value.astype(BF16)
@@ -151,45 +160,55 @@
     eye = (
         lax.broadcasted_iota(jnp.int32, (ch, ch), 0) == lax.broadcasted_iota(jnp.int32, (ch, ch), 1)
     ).astype(F32)
-    centre = w[0, 4 * ch : 5 * ch, :]
     half = ch // nb
     mine = pl.ds(pl.multiple_of(half * b, half), half)
     other = pl.ds(pl.multiple_of(half * (1 - b), half), half)
 
     def mats(level, buf, index, size, to):
+        near = [k for k in range(1, size) if ring(k, size) <= 2]
+        near.sort(key=lambda k: -ring(k, size))
+        far = [k for k in range(1, size) if ring(k, size) > 2]
+
+        def from_step(k):
+            return lax.rem(index - k + size, size)
+
+        def move(source, k, target):
+            return copy(
+                buf.at[source, mine], buf.at[source, mine], mat_s.at[level], mat_r.at[level, k], target
+            )
+
+        def swap(source):
+            return copy(buf.at[source, mine], buf.at[source, mine], pair_s.at[level], pair_r.at[level], partner)
+
         def start():
-            for k in range(1, size):
-                copy(
-                    buf.at[index, mine], buf.at[index, mine], mat_s.at[level, k], mat_r.at[level, k],
-                    to(lax.rem(index + k, size)),
-                ).start()
+            for k in near:
+                move(index, k, to(lax.rem(index + k, size))).start()
 
         def relay():
-            for k in range(1, size):
-                source = lax.rem(index - k + size, size)
-                copy(
-                    buf.at[source, mine], buf.at[source, mine], mat_s.at[level, k], mat_r.at[level, k], partner
-                ).wait_recv()
-                copy(
-                    buf.at[source, mine], buf.at[source, mine], pair_s.at[level, k], pair_r.at[level, k], partner
-                ).start()
+            for k in near:
+                source = from_step(k)
+                move(source, k, partner).wait_recv()
+                for f in far:
+                    through = 2 if f <= size // 2 else size - 2
+                    if k == through:
+                        move(source, f, to(lax.rem(index + f - k + size, size))).start()
+                swap(source).start()
+            for f in far:
+                source = from_step(f)
+                move(source, f, partner).wait_recv()
+                swap(source).start()
+
+        def all_of():
+            return buf.at[0 : size - 1, mine]
 
         def finish():
-            for k in range(1, size):
-                source = lax.rem(index - k + size, size)
-                copy(
-                    buf.at[source, other], buf.at[source, other], pair_s.at[level, k], pair_r.at[level, k], partner
-                ).wait_recv()
+            if size > 1:
+                copy(all_of(), all_of(), pair_s.at[level], pair_r.at[level], partner).wait_recv()
 
         def drain():
-            for k in range(1, size):
-                source = lax.rem(index - k + size, size)
-                copy(
-                    buf.at[index, mine], buf.at[index, mine], mat_s.at[level, k], mat_r.at[level, k], partner
-                ).wait_send()
-                copy(
-                    buf.at[source, mine], buf.at[source, mine], pair_s.at[level, k], pair_r.at[level, k], partner
-                ).wait_send()
+            if size > 1:
+                copy(all_of(), all_of(), mat_s.at[level], pair_r.at[level], partner).wait_send()
+                copy(all_of(), all_of(), pair_s.at[level], pair_r.at[level], partner).wait_send()
 
         return start, relay, finish, drain
 
@@ -197,9 +216,12 @@
     column_mats = mats(1, ry, y, ny, lambda t: (z, t, x, b))
     z_mats = mats(2, pz, z, nz, lambda t: (t, y, x, b))
 
-    kx[x] = centre.astype(F32)
+    loads[0].wait()
+    kx[x] = middle[...].astype(F32)
     pl.semaphore_wait(barrier, greeted)
     row_mats[0]()
+    for c in loads[1:]:
+        c.wait()
     relaxed = relax(states[...])
     shift_src[0] = relaxed
     forward_shift = copy(shift_src.at[0], shift_dst.at[0], shift_s.at[0], shift_r.at[0], ahead)
@@ -207,27 +229,43 @@
 
     row_mats[1]()
     row_mats[2]()
+    def step_map(j):
+        return eye + coarse_step * kx[j]
+
+    middle_x = (nx + 1) // 2
     pm[0] = eye
-    for j in range(nx):
-        pm[j + 1] = pm[j] + coarse_step * times_exact(pm[j], kx[j].astype(BF16))
     sm[nx - 1] = eye
-    for j in range(nx - 1, 0, -1):
-        sm[j - 1] = sm[j] + coarse_step * exact_times(kx[j].astype(BF16), sm[j])
-    ry[y] = pm[nx]
+
+    def row_sooner_map(j):
+        pm[j] = step_map(0) if j == 1 else pm[j - 1] + coarse_step * times_exact(pm[j - 1], kx[j - 1].astype(BF16))
+
+    def row_later_map(j):
+        first_later = step_map(j + 1)
+        sm[j] = first_later if j == nx - 2 else sm[j + 1] + coarse_step * exact_times(kx[j + 1].astype(BF16), sm[j + 1])
+
+    for j in range(1, middle_x + 1):
+        row_sooner_map(j)
+    for j in range(nx - 2, middle_x - 2, -1):
+        row_later_map(j)
+    ry[y] = times(pm[middle_x], sm[middle_x - 1]) if nx > 1 else pm[1]
     column_mats[0]()
+    for j in range(middle_x + 1, nx):
+        row_sooner_map(j)
+    for j in range(middle_x - 2, -1, -1):
+        row_later_map(j)
 
     def coarse_of(field, flip):
-        return field + coarse_step * times_exact(field, centre, flip)
+        return field + coarse_step * times_exact(field, middle[...], flip)
 
     def scan(d, extra_up, extra_z):
         flip = d == 1
         row_later, row_sooner = (pm, sm) if flip else (sm, pm)
         column_later, column_sooner = (pr, sr) if flip else (sr, pr)
         w_src[d] = times(c_buf[d], row_later[x], flip)
-        for k in range(1, plane):
-            t, to = mate(k)
+        for o in offsets:
+            _, t, to = mate(o)
             piece = pl.ds(pl.multiple_of(own_cells * t, own_cells), own_cells)
-            copy(w_src.at[d, piece], up.at[d, me], up_s.at[d, k], up_r.at[d, k], to).start()
+            copy(w_src.at[d, piece], up.at[d, me], up_s.at[d], up_r.at[d], to).start()
         own = pl.ds(pl.multiple_of(own_cells * me, own_cells), own_cells)
         up[d, me] = w_src[d, own]
 
@@ -251,14 +289,14 @@
 
         chain(0)
         extra_up()
-        for k in range(1, plane):
-            source = lax.rem(me - k + plane, plane)
-            copy(w_src.at[d, own], up.at[d, source], up_s.at[d, k], up_r.at[d, k], partner).wait_recv()
+        pieces = up.at[d, 0 : plane - 1]
+        if plane > 1:
+            copy(pieces, pieces, up_s.at[d], up_r.at[d], partner).wait_recv()
         row_total = [sum(up[d, r * nx + i] for i in range(nx)) for r in range(ny)]
         tz[d, z] = sum(times(row_total[r], column_later[r], flip) for r in range(ny))
-        for k in range(1, nz):
+        for k in z_steps:
             to = lax.rem(z + k, nz)
-            copy(tz.at[d, z], tz.at[d, z], z_s.at[d, k], z_r.at[d, k], (to, y, x, b)).start()
+            copy(tz.at[d, z], tz.at[d, z], z_s.at[d], z_r.at[d], (to, y, x, b)).start()
         inside = [None] * ny
         order = list(range(ny - 1, -1, -1)) if flip else list(range(ny))
         inside[order[0]] = jnp.zeros((own_cells, ch), F32)
@@ -266,9 +304,8 @@
             inside[s] = times(inside[r], ry[r], flip) + row_total[r]
         chain(1)
         extra_z()
-        for k in range(1, nz):
-            source = lax.rem(z - k + nz, nz)
-            copy(tz.at[d, source], tz.at[d, source], z_s.at[d, k], z_r.at[d, k], partner).wait_recv()
+        totals = tz.at[d, 0 : nz - 1]
+        copy(totals, totals, z_s.at[d], z_r.at[d], partner).wait_recv()
 
         def advance(k, s):
             i = nz - 1 - k if flip else k
@@ -277,36 +314,37 @@
         entering = lax.fori_loop(0, nz - 1 - z if flip else z, advance, jnp.zeros((own_cells, ch), F32))
         for r in range(ny):
             row_src[d, r] = times(entering, column_sooner[r], flip) + inside[r]
-        for k in range(1, plane):
-            t, to = mate(k)
-            copy(row_src.at[d, t // nx], down.at[d, own], down_s.at[d, k], down_r.at[d, k], to).start()
+        for o in offsets:
+            ty, _, to = mate(o)
+            copy(row_src.at[d, ty], down.at[d, own], down_s.at[d], down_r.at[d], to).start()
         down[d, own] = row_src[d, y]
         for k in range(2, nx - 1):
             chain(k)
-        for k in range(1, plane):
-            source = lax.rem(me - k + plane, plane)
-            piece = pl.ds(pl.multiple_of(own_cells * source, own_cells), own_cells)
-            copy(row_src.at[d, y], down.at[d, piece], down_s.at[d, k], down_r.at[d, k], partner).wait_recv()
+        if plane > 1:
+            copy(pieces, pieces, down_s.at[d], down_r.at[d], partner).wait_recv()
         results[d] = times(down[d], row_sooner[x], flip)
 
-        @pl.when(x == (0 if flip else nx - 1))
-        def _():
-            chain_copy().wait_recv()
-
-        @pl.when(x != (nx - 1 if flip else 0))
-        def _():
-            results[d] = results[d] + v_dst[d]
+        if nx > 1:
+
+            @pl.when(x == (0 if flip else nx - 1))
+            def _():
+                chain_copy().wait_recv()
+
+            @pl.when(x != (nx - 1 if flip else 0))
+            def _():
+                results[d] = results[d] + v_dst[d]
 
         def drain():
-            for k in range(1, plane):
-                copy(w_src.at[d, own], up.at[d, me], up_s.at[d, k], up_r.at[d, k], partner).wait_send()
-                copy(row_src.at[d, y], down.at[d, own], down_s.at[d, k], down_r.at[d, k], partner).wait_send()
-            for k in range(1, nz):
-                copy(tz.at[d, z], tz.at[d, z], z_s.at[d, k], z_r.at[d, k], partner).wait_send()
-
-            @pl.when(x != (0 if flip else nx - 1))
-            def _():
-                chain_copy().wait_send()
+            if plane > 1:
+                copy(pieces, pieces, up_s.at[d], up_r.at[d], partner).wait_send()
+                copy(pieces, pieces, down_s.at[d], down_r.at[d], partner).wait_send()
+            copy(totals, totals, z_s.at[d], z_r.at[d], partner).wait_send()
+
+            if nx > 1:
+
+                @pl.when(x != (0 if flip else nx - 1))
+                def _():
+                    chain_copy().wait_send()
 
         return drain
 
@@ -317,14 +355,26 @@
     def extra_up():
         column_mats[1]()
         column_mats[2]()
+        middle_y = (ny + 1) // 2
         pr[0] = eye
-        for j in range(ny):
-            pr[j + 1] = times(pr[j], ry[j])
         sr[ny - 1] = eye
-        for j in range(ny - 1, 0, -1):
-            sr[j - 1] = times(ry[j], sr[j])
-        pz[z] = pr[ny]
+
+        def sooner(j):
+            pr[j] = ry[0] if j == 1 else times(pr[j - 1], ry[j - 1])
+
+        def later(j):
+            sr[j] = ry[j + 1] if j == ny - 2 else times(ry[j + 1], sr[j + 1])
+
+        for j in range(1, middle_y + 1):
+            sooner(j)
+        for j in range(ny - 2, middle_y - 2, -1):
+            later(j)
+        pz[z] = times(pr[middle_y], sr[middle_y - 1]) if ny > 1 else pr[1]
         z_mats[0]()
+        for j in range(middle_y + 1, ny):
+            sooner(j)
+        for j in range(middle_y - 2, -1, -1):
+            later(j)
 
     def extra_z():
         z_mats[1]()
@@ -332,8 +382,7 @@
 
     forward_drain = scan(0, extra_up, extra_z)
     results[0] = jnp.where(first, states[...], results[0])
-    outs = [pltpu.make_async_copy(results.at[0], ns_out, out_sem.at[0])]
-    outs[0].start()
+    pltpu.make_async_copy(results.at[0], ns_out, out_sem.at[0]).start()
 
     def final_step(n, u):
         u_own[n] = u
@@ -350,8 +399,7 @@
     back_shift.start()
     new_ends = jnp.where(first, 0.0, coarse_of(results[0], False)) + c_buf[0]
     v_src[2] = new_ends
-    outs.append(pltpu.make_async_copy(v_src.at[2], ne_out, out_sem.at[1]))
-    outs[-1].start()
+    pltpu.make_async_copy(v_src.at[2], ne_out, out_sem.at[0]).start()
     for n in range(blocks):
         xt[n] = jnp.transpose(u_own[n]).astype(BF16)
     inputs_copy.wait_recv()
@@ -362,11 +410,10 @@
     c_buf[1] = jnp.where(final, 0.0, -coarse_of(back_start, True)) + back_relax(back_start)
     back_drain = scan(1, lambda: None, lambda: None)
     results[1] = jnp.where(final, guess[...], results[1])
-    outs.append(pltpu.make_async_copy(results.at[1], na_out, out_sem.at[2]))
-    outs[-1].start()
+    pltpu.make_async_copy(results.at[1], na_out, out_sem.at[0]).start()
 
     def sens_copy(n):
-        return copy(sens_own.at[n], sens_got.at[n], sens_s.at[n], sens_r.at[n], partner)
+        return copy(sens_own.at[n], sens_got.at[n], sens_s, sens_r.at[n], partner)
 
     def bias_sum(sens):
         return jnp.sum(sens.astype(BF16).astype(F32), axis=0, keepdims=True)
@@ -384,8 +431,7 @@
         g_own[n] = dot(xt[n], columns)
     new_back = jnp.where(final, 0.0, coarse_of(results[1], True)) + c_buf[1]
     v_src[3] = new_back
-    outs.append(pltpu.make_async_copy(v_src.at[3], nb_out, out_sem.at[3]))
-    outs[-1].start()
+    pltpu.make_async_copy(v_src.at[3], nb_out, out_sem.at[0]).start()
     factor = STEP / (nb * batch * cells)
     for n in range(blocks - 1, -1, -1):
         sens_copy(n).wait_recv()
@@ -394,13 +440,11 @@
         total = factor * (g_own[n] + dot(xt_got[n], patches()))
         for t in range(9):
             g_sum[n, t] = total[:, ch * (8 - t) : ch * (9 - t)]
-        outs.append(pltpu.make_async_copy(g_sum.at[n], gk_out.at[n], out_sem.at[4 + n]))
-        outs[-1].start()
-    outs.append(pltpu.make_async_copy(gb_sum, gb_out, out_sem.at[4 + blocks]))
-    outs[-1].start()
-
-    for n in range(blocks):
-        sens_copy(n).wait_send()
+        pltpu.make_async_copy(g_sum.at[n], gk_out.at[n], out_sem.at[1]).start()
+    bias_out = pltpu.make_async_copy(gb_sum, gb_out, out_sem.at[2])
+    bias_out.start()
+
+    copy(sens_own, sens_got, sens_s, u_r, partner).wait_send()
     inputs_copy.wait_send()
     forward_shift.wait_send()
     back_shift.wait_send()
@@ -409,8 +453,9 @@
     z_mats[3]()
     forward_drain()
     back_drain()
-    for c in outs:
-        c.wait()
+    pltpu.make_async_copy(v_src, v_src, out_sem.at[0]).wait()
+    pltpu.make_async_copy(g_sum, gk_out, out_sem.at[1]).wait()
+    bias_out.wait()
 
 
 def flush(*refs):
@@ -439,6 +484,7 @@
         vmem((blocks, ch), F32),
         vmem((cells, ch), F32),
         vmem((cells, ch), F32),
+        vmem((ch, ch), BF16),
         vmem((3, cells + 2 * side, ch), BF16),
         vmem((blocks, ch, cells), BF16),
         vmem((blocks, cells, ch), F32),
@@ -469,25 +515,25 @@
         vmem((blocks, ch, taps * ch), F32),
         vmem((blocks, taps, ch, ch), F32),
         vmem((blocks, ch), F32),
-        dma((3 + blocks,)),
-        dma((5 + blocks,)),
+        dma((5,)),
+        dma((3,)),
+        dma((3,)),
         dma((3, most)),
-        dma((3, most)),
-        dma((3, most)),
-        dma((3, most)),
-        dma((2,)),
-        dma((2,)),
-        dma((2,)),
-        dma((2,)),
-        dma((2, plane)),
-        dma((2, plane)),
-        dma((2, nz)),
-        dma((2, nz)),
-        dma((2, plane)),
-        dma((2, plane)),
+        dma((3,)),
+        dma((3,)),
+        dma((2,)),
+        dma((2,)),
+        dma((2,)),
+        dma((2,)),
+        dma((2,)),
+        dma((2,)),
+        dma((2,)),
+        dma((2,)),
+        dma((2,)),
+        dma((2,)),
         dma(()),
         dma(()),
-        dma((blocks,)),
+        dma(()),
         dma((blocks,)),
     ]
     any_space = pl.BlockSpec(memory_space=pl.ANY)

time: 77.1 us -> 72.2 us (0.936)
  Pallas kernels: 76.4 us -> 71.5 us
    pallas_call x1, Pallas kernels: 74.7 us -> 69.8 us  [body(): pl.pallas_call(functools.partial(kernel, sizes, blocks, side, batch), out...]
where the time goes in v3:
time: 72.2 us; the launch traced here: 72.1 us
  Pallas kernels  71.5 us (99%)
    pallas_call x1, Pallas kernels, body(): pl.pallas_call(functools.partial(kernel, sizes, blocks, side, batch), out...  69.8 us
    pallas_call x1, Pallas kernels, body(): pl.pallas_call(flush, out_shape=[jax.ShapeDtypeStruct(out.shape, out.dtyp...  1.64 us

profile of v3, /device:TPU:1, one launch (start us, length us, event | category | flops | bytes accessed | tf_op | source)
XLA Modules:
  0.0 72.1 jit_solution(3435847768005373328)
XLA Ops:
  0.6 69.8 %vcycle.1 = (f32[256,128]{1,0:T(8,128)S(1)}, f32[256,128]{1,0:T(8,128)S(1)}, f32[256,128]{1,0:T(8,128)S(1)}, f32[256,128]{1,0:T(8,128)S(1)}, f32[4,9,128,128]{3,2,1,0:T(8,128)S(1)}, /*index=5*/f32[4,128]{1,0:T(4,128)S(1)}) custom-call(bf16[4,1152,128]{2,1,0:T(8,128)(2,1)} %bitcast.7, f32[4,128]{1,0:T(4,128)} %b_hbm.1, f32[256,128]{1,0:T(8,128)} %bitcast.8, ...), custom_call_target="tpu_custom_call" | custom-call | tf_op jit(solution)/shard_map/vcycle/pallas_call | solution.py:540
  70.5 1.6 %flush.1 = (f32[256,128]{1,0:T(8,128)}, f32[256,128]{1,0:T(8,128)}, f32[256,128]{1,0:T(8,128)}, f32[256,128]{1,0:T(8,128)}, f32[4,9,128,128]{3,2,1,0:T(8,128)}, /*index=5*/f32[4,128]{1,0:T(4,128)}) custom-call(f32[256,128]{1,0:T(8,128)S(1)} %get-tuple-element.18.refs_0_, f32[256,128]{1,0:T(8,128)S(1)} %get-tuple-element.19.refs_1_, ...), custom_call_target="tpu_custom_call" | custom-call | tf_op jit(solution)/shard_map/flush/pallas_call | solution.py:562

commit v4 on v3

--- a/solution.py
+++ b/solution.py
@@ -50,10 +50,10 @@
     xs, xt, slopes,
     kx, ry, pz, pm, sm, pr, sr,
     shift_src, shift_dst, c_buf, v_src, v_dst,
-    w_src, up, tz, row_src, down, results, lam_ref,
+    w_src, up, tz, entering, row_src, down, results, lam_ref,
     u_own, u_got, xt_got, sens_own, sens_got, g_own, g_sum, gb_sum,
     in_sem, out_sem,
-    mat_s, mat_r, pair_s, pair_r,
+    mat_s, x_r, xp_r, y_r, yp_r, zm_r, zp_r,
     shift_s, shift_r, chain_s, chain_r,
     up_s, up_r, z_s, z_r, down_s, down_r,
     u_s, u_r, sens_s, sens_r,
@@ -121,30 +121,49 @@
         greet((lax.rem(z + k, nz), y, x, b))
     greeted = 3 + plane - 1 + nz - 1
 
-    for d in range(3):
-        xs[d, 0:side, :] = jnp.zeros((side, ch), BF16)
-        xs[d, side + cells : 2 * side + cells, :] = jnp.zeros((side, ch), BF16)
+    xs[0:side, :] = jnp.zeros((side, ch), BF16)
+    xs[side + cells : 2 * side + cells, :] = jnp.zeros((side, ch), BF16)
     column = lax.rem(lax.broadcasted_iota(jnp.int32, (cells, ch), 0), side)
     inner_left = column != 0
     inner_right = column != side - 1
 
     def place(value):
-        xs[1, side : side + cells, :] = value.astype(BF16)
-        xs[0, side : side + cells, :] = jnp.where(inner_left, pltpu.roll(value, 1, 0), 0.0).astype(BF16)
-        xs[2, side : side + cells, :] = jnp.where(inner_right, pltpu.roll(value, cells - 1, 0), 0.0).astype(BF16)
-
-    def patches():
-        return jnp.concatenate(
-            [xs[dx, side * dy : side * dy + cells, :] for dy in range(3) for dx in range(3)], axis=1
-        )
+        xs[side : side + cells, :] = value.astype(BF16)
+
+    def rows_beside():
+        return [xs[side * dy : side * dy + cells, :] for dy in range(3)]
+
+    def from_left(value):
+        return jnp.where(inner_left, pltpu.roll(value, 1, 0), 0.0)
+
+    def from_right(value):
+        return jnp.where(inner_right, pltpu.roll(value, cells - 1, 0), 0.0)
+
+    def join_columns(wide):
+        return wide[:, ch : 2 * ch] + (from_left(wide[:, :ch]) + from_right(wide[:, 2 * ch :]))
+
+    def tap(n, t):
+        return w[n, ch * t : ch * (t + 1), :]
 
     def activate(n, u):
         place(u)
-        return jnp.tanh(dot(patches(), w[n]) + bias[pl.ds(n, 1), :])
-
-    def adjoint_conv(n, columns):
-        flipped = jnp.concatenate([w[n, ch * (8 - t) : ch * (9 - t), :] for t in range(9)], axis=1)
-        return dot(columns, flipped, True)
+        weights = jnp.concatenate(
+            [jnp.concatenate([tap(n, 3 * dy + dx) for dx in range(3)], axis=1) for dy in range(3)], axis=0
+        )
+        wide = dot(jnp.concatenate(rows_beside(), axis=1), weights)
+        return jnp.tanh(join_columns(wide) + bias[pl.ds(n, 1), :])
+
+    def adjoint_conv(n):
+        flipped = jnp.concatenate(
+            [jnp.concatenate([tap(n, 8 - 3 * dy - dx) for dy in range(3)], axis=1) for dx in range(3)], axis=0
+        )
+        return join_columns(dot(jnp.concatenate(rows_beside(), axis=1), flipped, True))
+
+    def grad_product(inputs):
+        return dot(inputs, jnp.concatenate(rows_beside()[::-1], axis=1))
+
+    def beside(u):
+        return jnp.concatenate([jnp.transpose(v).astype(BF16) for v in (from_left(u), u, from_right(u))], axis=0)
 
     def relax(u):
         return lax.fori_loop(0, blocks, lambda n, s: s + STEP * activate(n, s), u)
@@ -153,7 +172,7 @@
         def body(k, lam):
             n = blocks - 1 - k
             place(slopes[n] * lam)
-            return lam + STEP * adjoint_conv(n, patches())
+            return lam + STEP * adjoint_conv(n)
 
         return lax.fori_loop(0, blocks, body, lam)
 
@@ -164,62 +183,64 @@
     mine = pl.ds(pl.multiple_of(half * b, half), half)
     other = pl.ds(pl.multiple_of(half * (1 - b), half), half)
 
-    def mats(level, buf, index, size, to):
-        near = [k for k in range(1, size) if ring(k, size) <= 2]
-        near.sort(key=lambda k: -ring(k, size))
-        far = [k for k in range(1, size) if ring(k, size) > 2]
-
-        def from_step(k):
-            return lax.rem(index - k + size, size)
-
-        def move(source, k, target):
-            return copy(
-                buf.at[source, mine], buf.at[source, mine], mat_s.at[level], mat_r.at[level, k], target
-            )
-
-        def swap(source):
-            return copy(buf.at[source, mine], buf.at[source, mine], pair_s.at[level], pair_r.at[level], partner)
-
-        def start():
-            for k in near:
-                move(index, k, to(lax.rem(index + k, size))).start()
-
-        def relay():
-            for k in near:
-                source = from_step(k)
-                move(source, k, partner).wait_recv()
-                for f in far:
-                    through = 2 if f <= size // 2 else size - 2
-                    if k == through:
-                        move(source, f, to(lax.rem(index + f - k + size, size))).start()
-                swap(source).start()
-            for f in far:
-                source = from_step(f)
-                move(source, f, partner).wait_recv()
-                swap(source).start()
-
-        def all_of():
-            return buf.at[0 : size - 1, mine]
-
-        def finish():
-            if size > 1:
-                copy(all_of(), all_of(), pair_s.at[level], pair_r.at[level], partner).wait_recv()
-
-        def drain():
-            if size > 1:
-                copy(all_of(), all_of(), mat_s.at[level], pair_r.at[level], partner).wait_send()
-                copy(all_of(), all_of(), pair_s.at[level], pair_r.at[level], partner).wait_send()
-
-        return start, relay, finish, drain
-
-    row_mats = mats(0, kx, x, nx, lambda t: (z, y, t, b))
-    column_mats = mats(1, ry, y, ny, lambda t: (z, t, x, b))
-    z_mats = mats(2, pz, z, nz, lambda t: (t, y, x, b))
+    class Maps:
+        def __init__(self, buf, index, size, to, send, recv, pair_send, pair_recv):
+            self.buf, self.index, self.size, self.to = buf, index, size, to
+            self.send, self.recv, self.pair_send, self.pair_recv = send, recv, pair_send, pair_recv
+            near = [k for k in range(1, size) if ring(k, size) <= 2]
+            near.sort(key=lambda k: -ring(k, size))
+            far = [k for k in range(size - 1, 0, -1) if ring(k, size) > 2]
+            self.near, self.far = near, far
+
+        def source(self, k):
+            return lax.rem(self.index - k + self.size, self.size)
+
+        def move(self, source, k, target):
+            part = self.buf.at[source, mine]
+            return copy(part, part, self.send, self.recv.at[k], target)
+
+        def swap(self, source, k, rows):
+            part = self.buf.at[source, rows]
+            return copy(part, part, self.pair_send, self.pair_recv.at[k], partner)
+
+        def start(self):
+            for k in self.near:
+                self.move(self.index, k, self.to(lax.rem(self.index + k, self.size))).start()
+
+        def pass_on(self, wanted=None, near=True, far=True):
+            for k in (self.near if near else []) + (self.far if far else []):
+                source = self.source(k)
+
+                def take(k=k, source=source):
+                    self.move(source, k, partner).wait_recv()
+                    for f in self.far:
+                        if k == (2 if f <= self.size // 2 else self.size - 2):
+                            self.move(source, f, self.to(lax.rem(self.index + f - k + self.size, self.size))).start()
+                    self.swap(source, k, mine).start()
+
+                if wanted is None:
+                    take()
+                else:
+                    pl.when(wanted(k, source))(take)
+
+        def finish(self):
+            for k in range(1, self.size):
+                self.swap(self.source(k), k, other).wait_recv()
+
+        def drain(self):
+            if self.size > 1:
+                part = self.buf.at[0 : self.size - 1, mine]
+                copy(part, part, self.send, self.recv.at[0], partner).wait_send()
+                copy(part, part, self.pair_send, self.recv.at[0], partner).wait_send()
+
+    row_mats = Maps(kx, x, nx, lambda t: (z, y, t, b), mat_s.at[0], x_r, mat_s.at[1], xp_r)
+    column_mats = Maps(ry, y, ny, lambda t: (z, t, x, b), mat_s.at[2], y_r, mat_s.at[3], yp_r)
+    z_mats = Maps(pz, z, nz, lambda t: (t, y, x, b), mat_s.at[4], zm_r, mat_s.at[5], zp_r)
 
     loads[0].wait()
     kx[x] = middle[...].astype(F32)
     pl.semaphore_wait(barrier, greeted)
-    row_mats[0]()
+    row_mats.start()
     for c in loads[1:]:
         c.wait()
     relaxed = relax(states[...])
@@ -227,8 +248,8 @@
     forward_shift = copy(shift_src.at[0], shift_dst.at[0], shift_s.at[0], shift_r.at[0], ahead)
     forward_shift.start()
 
-    row_mats[1]()
-    row_mats[2]()
+    row_mats.pass_on()
+    row_mats.finish()
     def step_map(j):
         return eye + coarse_step * kx[j]
 
@@ -248,16 +269,23 @@
     for j in range(nx - 2, middle_x - 2, -1):
         row_later_map(j)
     ry[y] = times(pm[middle_x], sm[middle_x - 1]) if nx > 1 else pm[1]
-    column_mats[0]()
+    column_mats.start()
     for j in range(middle_x + 1, nx):
         row_sooner_map(j)
     for j in range(middle_x - 2, -1, -1):
         row_later_map(j)
 
+    def early(k, source):
+        needed = (source < z) & (source != 0)
+        return needed | (z == 0) if k == nz - 2 and nz > 4 else needed
+
+    def late(k, source):
+        return jnp.logical_not(early(k, source))
+
     def coarse_of(field, flip):
         return field + coarse_step * times_exact(field, middle[...], flip)
 
-    def scan(d, extra_up, extra_z):
+    def scan(d, extra_up):
         flip = d == 1
         row_later, row_sooner = (pm, sm) if flip else (sm, pm)
         column_later, column_sooner = (pr, sr) if flip else (sr, pr)
@@ -296,30 +324,43 @@
         tz[d, z] = sum(times(row_total[r], column_later[r], flip) for r in range(ny))
         for k in z_steps:
             to = lax.rem(z + k, nz)
-            copy(tz.at[d, z], tz.at[d, z], z_s.at[d], z_r.at[d], (to, y, x, b)).start()
+            copy(tz.at[d, z], tz.at[d, z], z_s.at[d], z_r.at[d, k], (to, y, x, b)).start()
         inside = [None] * ny
         order = list(range(ny - 1, -1, -1)) if flip else list(range(ny))
         inside[order[0]] = jnp.zeros((own_cells, ch), F32)
         for r, s in zip(order, order[1:]):
             inside[s] = times(inside[r], ry[r], flip) + row_total[r]
         chain(1)
-        extra_z()
-        totals = tz.at[d, 0 : nz - 1]
-        copy(totals, totals, z_s.at[d], z_r.at[d], partner).wait_recv()
-
-        def advance(k, s):
-            i = nz - 1 - k if flip else k
-            return times(s, pz[i], flip) + tz[d, i]
-
-        entering = lax.fori_loop(0, nz - 1 - z if flip else z, advance, jnp.zeros((own_cells, ch), F32))
+        if not flip:
+            z_mats.pass_on(early)
+
+        def total_from(k):
+            source = lax.rem(z - k + nz, nz)
+            return copy(tz.at[d, source], tz.at[d, source], z_s.at[d], z_r.at[d, k], partner)
+
+        entering[...] = jnp.zeros((own_cells, ch), F32)
+        for i in range(nz - 1, 0, -1) if flip else range(nz - 1):
+
+            @pl.when(z < i if flip else z > i)
+            def _():
+                k = lax.rem(z - i + nz, nz)
+                total_from(k).wait_recv()
+                if i == (nz - 1 if flip else 0):
+                    entering[...] = tz[d, i]
+                else:
+                    z_mats.swap(i, k, other).wait_recv()
+                    entering[...] = times(entering[...], pz[i], flip) + tz[d, i]
+
         for r in range(ny):
-            row_src[d, r] = times(entering, column_sooner[r], flip) + inside[r]
+            row_src[d, r] = times(entering[...], column_sooner[r], flip) + inside[r]
         for o in offsets:
             ty, _, to = mate(o)
             copy(row_src.at[d, ty], down.at[d, own], down_s.at[d], down_r.at[d], to).start()
         down[d, own] = row_src[d, y]
         for k in range(2, nx - 1):
             chain(k)
+        if not flip:
+            z_mats.pass_on(late, far=False)
         if plane > 1:
             copy(pieces, pieces, down_s.at[d], down_r.at[d], partner).wait_recv()
         results[d] = times(down[d], row_sooner[x], flip)
@@ -338,7 +379,14 @@
             if plane > 1:
                 copy(pieces, pieces, up_s.at[d], up_r.at[d], partner).wait_send()
                 copy(pieces, pieces, down_s.at[d], down_r.at[d], partner).wait_send()
-            copy(totals, totals, z_s.at[d], z_r.at[d], partner).wait_send()
+            totals = tz.at[d, 0 : nz - 1]
+            copy(totals, totals, z_s.at[d], z_r.at[d, 0], partner).wait_send()
+            for i in range(nz):
+
+                @pl.when(z > i if flip else z < i)
+                def _():
+                    k = lax.rem(z - i + nz, nz)
+                    total_from(k).wait_recv()
 
             if nx > 1:
 
@@ -353,8 +401,8 @@
     c_buf[0] = jnp.where(first, 0.0, -coarse_of(start, False)) + relax(start)
 
     def extra_up():
-        column_mats[1]()
-        column_mats[2]()
+        column_mats.pass_on()
+        column_mats.finish()
         middle_y = (ny + 1) // 2
         pr[0] = eye
         sr[ny - 1] = eye
@@ -370,17 +418,13 @@
         for j in range(ny - 2, middle_y - 2, -1):
             later(j)
         pz[z] = times(pr[middle_y], sr[middle_y - 1]) if ny > 1 else pr[1]
-        z_mats[0]()
+        z_mats.start()
         for j in range(middle_y + 1, ny):
             sooner(j)
         for j in range(middle_y - 2, -1, -1):
             later(j)
 
-    def extra_z():
-        z_mats[1]()
-        z_mats[2]()
-
-    forward_drain = scan(0, extra_up, extra_z)
+    forward_drain = scan(0, extra_up)
     results[0] = jnp.where(first, states[...], results[0])
     pltpu.make_async_copy(results.at[0], ns_out, out_sem.at[0]).start()
 
@@ -401,14 +445,15 @@
     v_src[2] = new_ends
     pltpu.make_async_copy(v_src.at[2], ne_out, out_sem.at[0]).start()
     for n in range(blocks):
-        xt[n] = jnp.transpose(u_own[n]).astype(BF16)
+        xt[n] = beside(u_own[n])
     inputs_copy.wait_recv()
     for n in range(blocks):
-        xt_got[n] = jnp.transpose(u_got[n]).astype(BF16)
+        xt_got[n] = beside(u_got[n])
+    z_mats.pass_on(late, near=False)
     back_shift.wait_recv()
     back_start = jnp.where(final, guess[...], shift_dst[1])
     c_buf[1] = jnp.where(final, 0.0, -coarse_of(back_start, True)) + back_relax(back_start)
-    back_drain = scan(1, lambda: None, lambda: None)
+    back_drain = scan(1, lambda: None)
     results[1] = jnp.where(final, guess[...], results[1])
     pltpu.make_async_copy(results.at[1], na_out, out_sem.at[0]).start()
 
@@ -424,11 +469,10 @@
         sens_own[n] = sens
         sens_copy(n).start()
         place(sens)
-        columns = patches()
         if n > 0:
-            lam_ref[...] = lam_ref[...] + STEP * adjoint_conv(n, columns)
+            lam_ref[...] = lam_ref[...] + STEP * adjoint_conv(n)
         gb_sum[n : n + 1, :] = bias_sum(sens)
-        g_own[n] = dot(xt[n], columns)
+        g_own[n] = grad_product(xt[n])
     new_back = jnp.where(final, 0.0, coarse_of(results[1], True)) + c_buf[1]
     v_src[3] = new_back
     pltpu.make_async_copy(v_src.at[3], nb_out, out_sem.at[0]).start()
@@ -437,9 +481,10 @@
         sens_copy(n).wait_recv()
         place(sens_got[n])
         gb_sum[n : n + 1, :] = factor * (gb_sum[n : n + 1, :] + bias_sum(sens_got[n]))
-        total = factor * (g_own[n] + dot(xt_got[n], patches()))
-        for t in range(9):
-            g_sum[n, t] = total[:, ch * (8 - t) : ch * (9 - t)]
+        total = factor * (g_own[n] + grad_product(xt_got[n]))
+        for dy in range(3):
+            for dx in range(3):
+                g_sum[n, 3 * dy + dx] = total[ch * dx : ch * (dx + 1), ch * dy : ch * (dy + 1)]
         pltpu.make_async_copy(g_sum.at[n], gk_out.at[n], out_sem.at[1]).start()
     bias_out = pltpu.make_async_copy(gb_sum, gb_out, out_sem.at[2])
     bias_out.start()
@@ -448,9 +493,15 @@
     inputs_copy.wait_send()
     forward_shift.wait_send()
     back_shift.wait_send()
-    row_mats[3]()
-    column_mats[3]()
-    z_mats[3]()
+    row_mats.drain()
+    column_mats.drain()
+    z_mats.drain()
+    for i in {0, nz - 1}:
+
+        @pl.when(z != i)
+        def _():
+            z_mats.swap(i, lax.rem(z - i + nz, nz), other).wait_recv()
+
     forward_drain()
     back_drain()
     pltpu.make_async_copy(v_src, v_src, out_sem.at[0]).wait()
@@ -460,7 +511,9 @@
 
 def flush(*refs):
     sem = refs[-1]
-    copies = [pltpu.make_async_copy(refs[i], refs[6 + i], sem.at[i]) for i in range(6)]
+    blocks = refs[4].shape[0]
+    copies = [pltpu.make_async_copy(refs[4].at[n], refs[10].at[n], sem.at[n]) for n in range(blocks)]
+    copies += [pltpu.make_async_copy(refs[i], refs[6 + i], sem.at[blocks + i]) for i in (0, 1, 2, 3, 5)]
     for c in copies:
         c.start()
     for c in copies:
@@ -477,7 +530,6 @@
     own = cells // plane
     field = jax.ShapeDtypeStruct((cells, ch), F32)
     dma = pltpu.SemaphoreType.DMA
-    most = max(nz, ny, nx)
     vmem = pltpu.VMEM
     scratch = [
         vmem((blocks, taps * ch, ch), BF16),
@@ -485,8 +537,8 @@
         vmem((cells, ch), F32),
         vmem((cells, ch), F32),
         vmem((ch, ch), BF16),
-        vmem((3, cells + 2 * side, ch), BF16),
-        vmem((blocks, ch, cells), BF16),
+        vmem((cells + 2 * side, ch), BF16),
+        vmem((blocks, 3 * ch, cells), BF16),
         vmem((blocks, cells, ch), F32),
         vmem((nx, ch, ch), F32),
         vmem((ny, ch, ch), F32),
@@ -503,32 +555,36 @@
         vmem((2, cells, ch), F32),
         vmem((2, plane, own, ch), F32),
         vmem((2, nz, own, ch), F32),
+        vmem((own, ch), F32),
         vmem((2, ny, own, ch), F32),
         vmem((2, cells, ch), F32),
         vmem((2, cells, ch), F32),
         vmem((cells, ch), F32),
         vmem((blocks, cells, ch), F32),
         vmem((blocks, cells, ch), F32),
-        vmem((blocks, ch, cells), BF16),
+        vmem((blocks, 3 * ch, cells), BF16),
         vmem((blocks, cells, ch), F32),
         vmem((blocks, cells, ch), F32),
-        vmem((blocks, ch, taps * ch), F32),
+        vmem((blocks, 3 * ch, 3 * ch), F32),
         vmem((blocks, taps, ch, ch), F32),
         vmem((blocks, ch), F32),
         dma((5,)),
         dma((3,)),
-        dma((3,)),
-        dma((3, most)),
-        dma((3,)),
-        dma((3,)),
-        dma((2,)),
-        dma((2,)),
-        dma((2,)),
-        dma((2,)),
-        dma((2,)),
-        dma((2,)),
-        dma((2,)),
-        dma((2,)),
+        dma((6,)),
+        dma((nx,)),
+        dma((nx,)),
+        dma((ny,)),
+        dma((ny,)),
+        dma((nz,)),
+        dma((nz,)),
+        dma((2,)),
+        dma((2,)),
+        dma((2,)),
+        dma((2,)),
+        dma((2,)),
+        dma((2,)),
+        dma((2,)),
+        dma((2, nz)),
         dma((2,)),
         dma((2,)),
         dma(()),
@@ -564,7 +620,7 @@
         out_shape=[jax.ShapeDtypeStruct(out.shape, out.dtype) for out in outs],
         in_specs=[any_space] * 6,
         out_specs=[pl.BlockSpec(memory_space=pltpu.HBM)] * 6,
-        scratch_shapes=[dma((6,))],
+        scratch_shapes=[dma((6 + blocks,))],
         compiler_params=pltpu.CompilerParams(vmem_limit_bytes=1024 * 1024),
         name="flush",
     )(*outs)

time: 72.2 us -> 70.4 us (0.975)
  Pallas kernels: 71.5 us -> 69.7 us
    pallas_call x1, Pallas kernels: 69.8 us -> 68 us  [body(): pl.pallas_call(functools.partial(kernel, sizes, blocks, side, batch), out...]
where the time goes in v4:
time: 70.4 us; the launch traced here: 70.3 us
  Pallas kernels  69.7 us (99%)
    pallas_call x1, Pallas kernels, body(): pl.pallas_call(functools.partial(kernel, sizes, blocks, side, batch), out...  68 us
    pallas_call x1, Pallas kernels, body(): pl.pallas_call(flush, out_shape=[jax.ShapeDtypeStruct(out.shape, out.dtyp...  1.65 us

profile of v4, /device:TPU:1, one launch (start us, length us, event | category | flops | bytes accessed | tf_op | source)
XLA Modules:
  0.0 70.3 jit_solution(14767173068601421356)
XLA Ops:
  0.6 68.0 %vcycle.1 = (f32[256,128]{1,0:T(8,128)S(1)}, f32[256,128]{1,0:T(8,128)S(1)}, f32[256,128]{1,0:T(8,128)S(1)}, f32[256,128]{1,0:T(8,128)S(1)}, f32[4,9,128,128]{3,2,1,0:T(8,128)S(1)}, /*index=5*/f32[4,128]{1,0:T(4,128)S(1)}) custom-call(bf16[4,1152,128]{2,1,0:T(8,128)(2,1)} %bitcast.7, f32[4,128]{1,0:T(4,128)} %b_hbm.1, f32[256,128]{1,0:T(8,128)} %bitcast.8, ...), custom_call_target="tpu_custom_call" | custom-call | tf_op jit(solution)/shard_map/vcycle/pallas_call | solution.py:596
  68.7 1.7 %flush.1 = (f32[256,128]{1,0:T(8,128)}, f32[256,128]{1,0:T(8,128)}, f32[256,128]{1,0:T(8,128)}, f32[256,128]{1,0:T(8,128)}, f32[4,9,128,128]{3,2,1,0:T(8,128)}, /*index=5*/f32[4,128]{1,0:T(4,128)}) custom-call(f32[256,128]{1,0:T(8,128)S(1)} %get-tuple-element.18.refs_0_, f32[256,128]{1,0:T(8,128)S(1)} %get-tuple-element.19.refs_1_, ...), custom_call_target="tpu_custom_call" | custom-call | tf_op jit(solution)/shard_map/flush/pallas_call | solution.py:618

commit v5 on v4

--- a/solution.py
+++ b/solution.py
@@ -43,15 +43,15 @@
 
 
 def kernel(
-    sizes, blocks, side, batch,
+    sizes, blocks, side,
     k_hbm, b_hbm, st_hbm, ad_hbm,
-    ns_out, ne_out, na_out, nb_out, gk_out, gb_out,
+    ns_out, ne_out, na_out, nb_out, xt_out, sens_out,
     w, bias, states, guess, middle,
     xs, xt, slopes,
     kx, ry, pz, pm, sm, pr, sr,
     shift_src, shift_dst, c_buf, v_src, v_dst,
     w_src, up, tz, entering, row_src, down, results, lam_ref,
-    u_own, u_got, xt_got, sens_own, sens_got, g_own, g_sum, gb_sum,
+    u_all, sens_all,
     in_sem, out_sem,
     mat_s, x_r, xp_r, y_r, yp_r, zm_r, zp_r,
     shift_s, shift_r, chain_s, chain_r,
@@ -123,6 +123,15 @@
 
     xs[0:side, :] = jnp.zeros((side, ch), BF16)
     xs[side + cells : 2 * side + cells, :] = jnp.zeros((side, ch), BF16)
+
+    @pl.when(first)
+    def _():
+        shift_dst[0] = jnp.zeros((cells, ch), F32)
+
+    @pl.when(final)
+    def _():
+        shift_dst[1] = jnp.zeros((cells, ch), F32)
+
     column = lax.rem(lax.broadcasted_iota(jnp.int32, (cells, ch), 0), side)
     inner_left = column != 0
     inner_right = column != side - 1
@@ -159,14 +168,11 @@
         )
         return join_columns(dot(jnp.concatenate(rows_beside(), axis=1), flipped, True))
 
-    def grad_product(inputs):
-        return dot(inputs, jnp.concatenate(rows_beside()[::-1], axis=1))
-
     def beside(u):
         return jnp.concatenate([jnp.transpose(v).astype(BF16) for v in (from_left(u), u, from_right(u))], axis=0)
 
     def relax(u):
-        return lax.fori_loop(0, blocks, lambda n, s: s + STEP * activate(n, s), u)
+        return lax.fori_loop(0, blocks, lambda n, s: s + STEP * activate(n, s), u, unroll=True)
 
     def back_relax(lam):
         def body(k, lam):
@@ -174,7 +180,7 @@
             place(slopes[n] * lam)
             return lam + STEP * adjoint_conv(n)
 
-        return lax.fori_loop(0, blocks, body, lam)
+        return lax.fori_loop(0, blocks, body, lam, unroll=True)
 
     eye = (
         lax.broadcasted_iota(jnp.int32, (ch, ch), 0) == lax.broadcasted_iota(jnp.int32, (ch, ch), 1)
@@ -237,16 +243,15 @@
     column_mats = Maps(ry, y, ny, lambda t: (z, t, x, b), mat_s.at[2], y_r, mat_s.at[3], yp_r)
     z_mats = Maps(pz, z, nz, lambda t: (t, y, x, b), mat_s.at[4], zm_r, mat_s.at[5], zp_r)
 
-    loads[0].wait()
+    for c in loads:
+        c.wait()
     kx[x] = middle[...].astype(F32)
+    relaxed = relax(states[...])
     pl.semaphore_wait(barrier, greeted)
     row_mats.start()
-    for c in loads[1:]:
-        c.wait()
-    relaxed = relax(states[...])
     shift_src[0] = relaxed
     forward_shift = copy(shift_src.at[0], shift_dst.at[0], shift_s.at[0], shift_r.at[0], ahead)
-    forward_shift.start()
+    pl.when(pos != last)(forward_shift.start)
 
     row_mats.pass_on()
     row_mats.finish()
@@ -315,8 +320,8 @@
                     v_src[d] = coarse_of(v_dst[d], flip) + c_buf[d]
                 chain_copy().start()
 
+        extra_up()
         chain(0)
-        extra_up()
         pieces = up.at[d, 0 : plane - 1]
         if plane > 1:
             copy(pieces, pieces, up_s.at[d], up_r.at[d], partner).wait_recv()
@@ -330,9 +335,9 @@
         inside[order[0]] = jnp.zeros((own_cells, ch), F32)
         for r, s in zip(order, order[1:]):
             inside[s] = times(inside[r], ry[r], flip) + row_total[r]
-        chain(1)
         if not flip:
             z_mats.pass_on(early)
+        chain(1)
 
         def total_from(k):
             source = lax.rem(z - k + nz, nz)
@@ -396,7 +401,7 @@
 
         return drain
 
-    forward_shift.wait_recv()
+    pl.when(pos != 0)(forward_shift.wait_recv)
     start = jnp.where(first, states[...], shift_dst[0])
     c_buf[0] = jnp.where(first, 0.0, -coarse_of(start, False)) + relax(start)
 
@@ -429,28 +434,29 @@
     pltpu.make_async_copy(results.at[0], ns_out, out_sem.at[0]).start()
 
     def final_step(n, u):
-        u_own[n] = u
+        u_all[b, n] = u
         activ = activate(n, u)
         slopes[n] = 1.0 - activ * activ
         return u + STEP * activ
 
-    lax.fori_loop(0, blocks, final_step, results[0])
-    inputs_copy = copy(u_own, u_got, u_s, u_r, partner)
+    lax.fori_loop(0, blocks, final_step, results[0], unroll=True)
+    inputs_copy = copy(u_all.at[b], u_all.at[b], u_s, u_r, partner)
     inputs_copy.start()
 
     shift_src[1] = back_relax(guess[...])
     back_shift = copy(shift_src.at[1], shift_dst.at[1], shift_s.at[1], shift_r.at[1], behind)
-    back_shift.start()
+    pl.when(pos != 0)(back_shift.start)
     new_ends = jnp.where(first, 0.0, coarse_of(results[0], False)) + c_buf[0]
     v_src[2] = new_ends
     pltpu.make_async_copy(v_src.at[2], ne_out, out_sem.at[0]).start()
-    for n in range(blocks):
-        xt[n] = beside(u_own[n])
     inputs_copy.wait_recv()
     for n in range(blocks):
-        xt_got[n] = beside(u_got[n])
+        for i in range(nb):
+            xt[n, :, cells * i : cells * (i + 1)] = beside(u_all[i, n])
+    inputs_out = pltpu.make_async_copy(xt, xt_out, out_sem.at[1])
+    inputs_out.start()
     z_mats.pass_on(late, near=False)
-    back_shift.wait_recv()
+    pl.when(pos != last)(back_shift.wait_recv)
     back_start = jnp.where(final, guess[...], shift_dst[1])
     c_buf[1] = jnp.where(final, 0.0, -coarse_of(back_start, True)) + back_relax(back_start)
     back_drain = scan(1, lambda: None)
@@ -458,41 +464,28 @@
     pltpu.make_async_copy(results.at[1], na_out, out_sem.at[0]).start()
 
     def sens_copy(n):
-        return copy(sens_own.at[n], sens_got.at[n], sens_s, sens_r.at[n], partner)
-
-    def bias_sum(sens):
-        return jnp.sum(sens.astype(BF16).astype(F32), axis=0, keepdims=True)
+        return copy(sens_all.at[n, b], sens_all.at[n, b], sens_s, sens_r.at[n], partner)
 
     lam_ref[...] = results[1]
     for n in range(blocks - 1, -1, -1):
         sens = slopes[n] * lam_ref[...]
-        sens_own[n] = sens
+        sens_all[n, b] = sens
         sens_copy(n).start()
-        place(sens)
         if n > 0:
+            place(sens)
             lam_ref[...] = lam_ref[...] + STEP * adjoint_conv(n)
-        gb_sum[n : n + 1, :] = bias_sum(sens)
-        g_own[n] = grad_product(xt[n])
     new_back = jnp.where(final, 0.0, coarse_of(results[1], True)) + c_buf[1]
     v_src[3] = new_back
     pltpu.make_async_copy(v_src.at[3], nb_out, out_sem.at[0]).start()
-    factor = STEP / (nb * batch * cells)
     for n in range(blocks - 1, -1, -1):
-        sens_copy(n).wait_recv()
-        place(sens_got[n])
-        gb_sum[n : n + 1, :] = factor * (gb_sum[n : n + 1, :] + bias_sum(sens_got[n]))
-        total = factor * (g_own[n] + grad_product(xt_got[n]))
-        for dy in range(3):
-            for dx in range(3):
-                g_sum[n, 3 * dy + dx] = total[ch * dx : ch * (dx + 1), ch * dy : ch * (dy + 1)]
-        pltpu.make_async_copy(g_sum.at[n], gk_out.at[n], out_sem.at[1]).start()
-    bias_out = pltpu.make_async_copy(gb_sum, gb_out, out_sem.at[2])
-    bias_out.start()
-
-    copy(sens_own, sens_got, sens_s, u_r, partner).wait_send()
+        got = sens_all.at[n, 1 - b]
+        copy(got, got, sens_s, sens_r.at[n], partner).wait_recv()
+        pltpu.make_async_copy(sens_all.at[n], sens_out.at[n], out_sem.at[2]).start()
+
+    copy(u_all.at[0], u_all.at[0], sens_s, u_r, partner).wait_send()
     inputs_copy.wait_send()
-    forward_shift.wait_send()
-    back_shift.wait_send()
+    pl.when(pos != last)(forward_shift.wait_send)
+    pl.when(pos != 0)(back_shift.wait_send)
     row_mats.drain()
     column_mats.drain()
     z_mats.drain()
@@ -505,18 +498,46 @@
     forward_drain()
     back_drain()
     pltpu.make_async_copy(v_src, v_src, out_sem.at[0]).wait()
-    pltpu.make_async_copy(g_sum, gk_out, out_sem.at[1]).wait()
-    bias_out.wait()
-
-
-def flush(*refs):
-    sem = refs[-1]
-    blocks = refs[4].shape[0]
-    copies = [pltpu.make_async_copy(refs[4].at[n], refs[10].at[n], sem.at[n]) for n in range(blocks)]
-    copies += [pltpu.make_async_copy(refs[i], refs[6 + i], sem.at[blocks + i]) for i in (0, 1, 2, 3, 5)]
-    for c in copies:
+    inputs_out.wait()
+    pltpu.make_async_copy(sens_all, sens_out, out_sem.at[2]).wait()
+
+
+def gradients(
+    factor, side,
+    ns, ne, na, nb, xt, sens,
+    ns_out, ne_out, na_out, nb_out, gk_out, gb_out,
+    xs, grads, bias_grads, out_sem,
+):
+    blocks, images, cells, ch = sens.shape
+    outs = [
+        pltpu.make_async_copy(a, out, out_sem.at[blocks + 1 + i])
+        for i, (a, out) in enumerate(((ns, ns_out), (ne, ne_out), (na, na_out), (nb, nb_out)))
+    ]
+    for c in outs:
         c.start()
-    for c in copies:
+    for i in range(images):
+        xs[i, 0:side, :] = jnp.zeros((side, ch), BF16)
+        xs[i, side + cells : 2 * side + cells, :] = jnp.zeros((side, ch), BF16)
+    for n in range(blocks):
+        bias_sum = jnp.zeros((1, ch), F32)
+        for i in range(images):
+            rounded = sens[n, i].astype(BF16)
+            xs[i, side : side + cells, :] = rounded
+            bias_sum = bias_sum + jnp.sum(rounded.astype(F32), axis=0, keepdims=True)
+        bias_grads[n : n + 1, :] = factor * bias_sum
+        rows = [
+            jnp.concatenate([xs[i, side * dy : side * dy + cells, :] for dy in (2, 1, 0)], axis=1)
+            for i in range(images)
+        ]
+        total = factor * dot(xt[n], jnp.concatenate(rows, axis=0))
+        for dy in range(3):
+            for dx in range(3):
+                grads[n, 3 * dy + dx] = total[ch * dx : ch * (dx + 1), ch * dy : ch * (dy + 1)]
+        outs.append(pltpu.make_async_copy(grads.at[n], gk_out.at[n], out_sem.at[n]))
+        outs[-1].start()
+    outs.append(pltpu.make_async_copy(bias_grads, gb_out, out_sem.at[blocks]))
+    outs[-1].start()
+    for c in outs:
         c.wait()
 
 
@@ -538,7 +559,7 @@
         vmem((cells, ch), F32),
         vmem((ch, ch), BF16),
         vmem((cells + 2 * side, ch), BF16),
-        vmem((blocks, 3 * ch, cells), BF16),
+        vmem((blocks, 3 * ch, nb * cells), BF16),
         vmem((blocks, cells, ch), F32),
         vmem((nx, ch, ch), F32),
         vmem((ny, ch, ch), F32),
@@ -560,14 +581,8 @@
         vmem((2, cells, ch), F32),
         vmem((2, cells, ch), F32),
         vmem((cells, ch), F32),
-        vmem((blocks, cells, ch), F32),
-        vmem((blocks, cells, ch), F32),
-        vmem((blocks, 3 * ch, cells), BF16),
-        vmem((blocks, cells, ch), F32),
-        vmem((blocks, cells, ch), F32),
-        vmem((blocks, 3 * ch, 3 * ch), F32),
-        vmem((blocks, taps, ch, ch), F32),
-        vmem((blocks, ch), F32),
+        vmem((nb, blocks, cells, ch), F32),
+        vmem((blocks, nb, cells, ch), F32),
         dma((5,)),
         dma((3,)),
         dma((6,)),
@@ -594,9 +609,12 @@
     ]
     any_space = pl.BlockSpec(memory_space=pl.ANY)
     outs = pl.pallas_call(
-        functools.partial(kernel, sizes, blocks, side, batch),
+        functools.partial(kernel, sizes, blocks, side),
         out_shape=[field] * 4
-        + [jax.ShapeDtypeStruct((blocks, taps, ch, ch), F32), jax.ShapeDtypeStruct((blocks, ch), F32)],
+        + [
+            jax.ShapeDtypeStruct((blocks, 3 * ch, nb * cells), BF16),
+            jax.ShapeDtypeStruct((blocks, nb, cells, ch), F32),
+        ],
         in_specs=[pl.BlockSpec(memory_space=pltpu.HBM)] * 4,
         out_specs=[any_space] * 6,
         scratch_shapes=scratch,
@@ -616,13 +634,19 @@
         )
     )
     outs = pl.pallas_call(
-        flush,
-        out_shape=[jax.ShapeDtypeStruct(out.shape, out.dtype) for out in outs],
-        in_specs=[any_space] * 6,
+        functools.partial(gradients, STEP / (nb * batch * cells), side),
+        out_shape=[field] * 4
+        + [jax.ShapeDtypeStruct((blocks, taps, ch, ch), F32), jax.ShapeDtypeStruct((blocks, ch), F32)],
+        in_specs=[any_space] * 4 + [pl.BlockSpec(memory_space=vmem)] * 2,
         out_specs=[pl.BlockSpec(memory_space=pltpu.HBM)] * 6,
-        scratch_shapes=[dma((6 + blocks,))],
-        compiler_params=pltpu.CompilerParams(vmem_limit_bytes=1024 * 1024),
-        name="flush",
+        scratch_shapes=[
+            vmem((nb, cells + 2 * side, ch), BF16),
+            vmem((blocks, taps, ch, ch), F32),
+            vmem((blocks, ch), F32),
+            dma((blocks + 5,)),
+        ],
+        compiler_params=pltpu.CompilerParams(vmem_limit_bytes=16 * 1024 * 1024),
+        name="gradients",
     )(*outs)
     fields = [out.reshape(states.shape) for out in outs[:4]]
     return (*fields, outs[4], outs[5])

time: 70.4 us -> 70 us (level)
  no operation moved by 1% of the time
where the time goes in v5:
time: 70 us; the launch traced here: 69.9 us
  Pallas kernels  69.2 us (99%)
    pallas_call x1, Pallas kernels, body(): pl.pallas_call(functools.partial(kernel, sizes, blocks, side), out_shape=...  67.3 us
    pallas_call x1, Pallas kernels, body(): pl.pallas_call(functools.partial(gradients, STEP / (nb * batch * cells),...  1.91 us

profile of v5, /device:TPU:1, one launch (start us, length us, event | category | flops | bytes accessed | tf_op | source)
XLA Modules:
  0.0 69.9 jit_solution(7215824953132677509)
XLA Ops:
  0.6 67.3 %vcycle.1 = (f32[256,128]{1,0:T(8,128)S(1)}, f32[256,128]{1,0:T(8,128)S(1)}, f32[256,128]{1,0:T(8,128)S(1)}, f32[256,128]{1,0:T(8,128)S(1)}, bf16[4,384,512]{2,1...) custom-call(bf16[4,1152,128]{2,1,0:T(8,128)(2,1)} %bitcast.7, f32[4,128]{1,0:T(4,128)} %b_hbm.1, f32[256,128]{1,0:T(8,128)} %bitcast.8, ...), custom_call_target="tpu_custom_call" | custom-call | tf_op jit(solution)/shard_map/vcycle/pallas_call | solution.py:611
  68.0 1.9 %gradients.1 = (f32[256,128]{1,0:T(8,128)}, f32[256,128]{1,0:T(8,128)}, f32[256,128]{1,0:T(8,128)}, f32[256,128]{1,0:T(8,128)}, f32[4,9,128,128]{3,2,1,0:T(8,128)}, /*index=5*/f32[4,128]{1,0:T(4,128)}) custom-call(f32[256,128]{1,0:T(8,128)S(1)} %get-tuple-element.18.ns, f32[256,128]{1,0:T(8,128)S(1)} %get-tuple-element.19.ne, ...), custom_call_target="tpu_custom_call" | custom-call | tf_op jit(solution)/shard_map/gradients/pallas_call | solution.py:636

commit v6 on v5

--- a/solution.py
+++ b/solution.py
@@ -97,14 +97,16 @@
             src_ref=src, dst_ref=dst, send_sem=send, recv_sem=recv, device_id=to, device_id_type=MESH
         )
 
-    loads = [
-        pltpu.make_async_copy(k_hbm.at[0, 4 * ch : 5 * ch], middle, in_sem.at[0]),
-        pltpu.make_async_copy(st_hbm, states, in_sem.at[1]),
-        pltpu.make_async_copy(b_hbm, bias, in_sem.at[2]),
-        pltpu.make_async_copy(k_hbm, w, in_sem.at[3]),
-        pltpu.make_async_copy(ad_hbm, guess, in_sem.at[4]),
+    weight_loads = [pltpu.make_async_copy(k_hbm.at[n], w.at[n], in_sem.at[4 + n]) for n in range(blocks)]
+    first_loads = [
+        pltpu.make_async_copy(st_hbm, states, in_sem.at[0]),
+        pltpu.make_async_copy(b_hbm, bias, in_sem.at[1]),
     ]
-    for c in loads:
+    later_loads = [
+        pltpu.make_async_copy(k_hbm.at[0, 4 * ch : 5 * ch], middle, in_sem.at[2]),
+        pltpu.make_async_copy(ad_hbm, guess, in_sem.at[3]),
+    ]
+    for c in (weight_loads[0], *first_loads, *weight_loads[1:], *later_loads):
         c.start()
 
     barrier = pltpu.get_barrier_semaphore()
@@ -243,10 +245,15 @@
     column_mats = Maps(ry, y, ny, lambda t: (z, t, x, b), mat_s.at[2], y_r, mat_s.at[3], yp_r)
     z_mats = Maps(pz, z, nz, lambda t: (t, y, x, b), mat_s.at[4], zm_r, mat_s.at[5], zp_r)
 
-    for c in loads:
+    for c in first_loads:
+        c.wait()
+    relaxed = states[...]
+    for n in range(blocks):
+        weight_loads[n].wait()
+        relaxed = relaxed + STEP * activate(n, relaxed)
+    for c in later_loads:
         c.wait()
     kx[x] = middle[...].astype(F32)
-    relaxed = relax(states[...])
     pl.semaphore_wait(barrier, greeted)
     row_mats.start()
     shift_src[0] = relaxed
@@ -330,13 +337,13 @@
         for k in z_steps:
             to = lax.rem(z + k, nz)
             copy(tz.at[d, z], tz.at[d, z], z_s.at[d], z_r.at[d, k], (to, y, x, b)).start()
+        if not flip:
+            z_mats.pass_on(early)
         inside = [None] * ny
         order = list(range(ny - 1, -1, -1)) if flip else list(range(ny))
         inside[order[0]] = jnp.zeros((own_cells, ch), F32)
         for r, s in zip(order, order[1:]):
             inside[s] = times(inside[r], ry[r], flip) + row_total[r]
-        if not flip:
-            z_mats.pass_on(early)
         chain(1)
 
         def total_from(k):
@@ -583,7 +590,7 @@
         vmem((cells, ch), F32),
         vmem((nb, blocks, cells, ch), F32),
         vmem((blocks, nb, cells, ch), F32),
-        dma((5,)),
+        dma((4 + blocks,)),
         dma((3,)),
         dma((6,)),
         dma((nx,)),

time: 70 us -> 69.9 us (level)
  no operation moved by 1% of the time
where the time goes in v6:
time: 69.9 us; the launch traced here: 69.8 us
  Pallas kernels  69.1 us (99%)
    pallas_call x1, Pallas kernels, body(): pl.pallas_call(functools.partial(kernel, sizes, blocks, side), out_shape=...  67.2 us
    pallas_call x1, Pallas kernels, body(): pl.pallas_call(functools.partial(gradients, STEP / (nb * batch * cells),...  1.9 us

profile of v6, /device:TPU:1, one launch (start us, length us, event | category | flops | bytes accessed | tf_op | source)
XLA Modules:
  0.0 69.8 jit_solution(10421949671582171087)
XLA Ops:
  0.6 67.2 %vcycle.1 = (f32[256,128]{1,0:T(8,128)S(1)}, f32[256,128]{1,0:T(8,128)S(1)}, f32[256,128]{1,0:T(8,128)S(1)}, f32[256,128]{1,0:T(8,128)S(1)}, bf16[4,384,512]{2,1...) custom-call(bf16[4,1152,128]{2,1,0:T(8,128)(2,1)} %bitcast.7, f32[4,128]{1,0:T(4,128)} %b_hbm.1, f32[256,128]{1,0:T(8,128)} %bitcast.8, ...), custom_call_target="tpu_custom_call" | custom-call | tf_op jit(solution)/shard_map/vcycle/pallas_call | solution.py:618
  67.9 1.9 %gradients.1 = (f32[256,128]{1,0:T(8,128)}, f32[256,128]{1,0:T(8,128)}, f32[256,128]{1,0:T(8,128)}, f32[256,128]{1,0:T(8,128)}, f32[4,9,128,128]{3,2,1,0:T(8,128)}, /*index=5*/f32[4,128]{1,0:T(4,128)}) custom-call(f32[256,128]{1,0:T(8,128)S(1)} %get-tuple-element.18.ns, f32[256,128]{1,0:T(8,128)S(1)} %get-tuple-element.19.ne, ...), custom_call_target="tpu_custom_call" | custom-call | tf_op jit(solution)/shard_map/gradients/pallas_call | solution.py:643

commit v7 on v6

--- a/solution.py
+++ b/solution.py
@@ -216,7 +216,8 @@
                 self.move(self.index, k, self.to(lax.rem(self.index + k, self.size))).start()
 
         def pass_on(self, wanted=None, near=True, far=True):
-            for k in (self.near if near else []) + (self.far if far else []):
+            order = self.near if self.far else self.near[::-1]
+            for k in (order if near else []) + (self.far if far else []):
                 source = self.source(k)
 
                 def take(k=k, source=source):

time: 69.9 us -> 70 us (level)
  no operation moved by 1% of the time
where the time goes in v7:
time: 70 us; the launch traced here: 69.9 us
  Pallas kernels  69.2 us (99%)
    pallas_call x1, Pallas kernels, body(): pl.pallas_call(functools.partial(kernel, sizes, blocks, side), out_shape=...  67.3 us
    pallas_call x1, Pallas kernels, body(): pl.pallas_call(functools.partial(gradients, STEP / (nb * batch * cells),...  1.9 us

profile of v7, /device:TPU:1, one launch (start us, length us, event | category | flops | bytes accessed | tf_op | source)
XLA Modules:
  0.0 69.9 jit_solution(11207699189973034388)
XLA Ops:
  0.6 67.3 %vcycle.1 = (f32[256,128]{1,0:T(8,128)S(1)}, f32[256,128]{1,0:T(8,128)S(1)}, f32[256,128]{1,0:T(8,128)S(1)}, f32[256,128]{1,0:T(8,128)S(1)}, bf16[4,384,512]{2,1...) custom-call(bf16[4,1152,128]{2,1,0:T(8,128)(2,1)} %bitcast.7, f32[4,128]{1,0:T(4,128)} %b_hbm.1, f32[256,128]{1,0:T(8,128)} %bitcast.8, ...), custom_call_target="tpu_custom_call" | custom-call | tf_op jit(solution)/shard_map/vcycle/pallas_call | solution.py:619
  67.9 1.9 %gradients.1 = (f32[256,128]{1,0:T(8,128)}, f32[256,128]{1,0:T(8,128)}, f32[256,128]{1,0:T(8,128)}, f32[256,128]{1,0:T(8,128)}, f32[4,9,128,128]{3,2,1,0:T(8,128)}, /*index=5*/f32[4,128]{1,0:T(4,128)}) custom-call(f32[256,128]{1,0:T(8,128)S(1)} %get-tuple-element.18.ns, f32[256,128]{1,0:T(8,128)S(1)} %get-tuple-element.19.ne, ...), custom_call_target="tpu_custom_call" | custom-call | tf_op jit(solution)/shard_map/gradients/pallas_call | solution.py:644
